TPU v7x, 512 devices: a whole 4x4x16 slice. The times are simulated.
512 devices in a mesh: leaf: 32 (over x, z_lo, core), col: 16 (over y, z_hi).
Axes of the slice: x: 4, y: 4, z: 16 (z_hi: 4, z_lo: 4; z = z_hi * 4 + z_lo), core: 2. Of those that a mesh axis runs over, the one named last changes fastest.
Arguments:
- right_sides: float32 [256, 65536], P('col', 'leaf'), may hold values from -6 to 6
- inverse_first: float32 [128, 128, 128], P('leaf'), may hold values from -0.5 to 0.5
- coupling_first: float32 [128, 3, 128, 128], P('leaf'), may hold values from -0.3125 to 0.3125
- links_first: int32 [128, 3], P('leaf'), may hold values from 0 to 11, as said below
- order_first: int32 [32, 12], P('leaf'), may hold values from 0 to 11, as said below
- inverse_second: float32 [128, 128, 128], P('leaf'), may hold values from -0.5 to 0.5
- coupling_second: float32 [128, 3, 128, 128], P('leaf'), may hold values from -0.3125 to 0.3125
- links_second: int32 [128, 3], P('leaf'), may hold values from 0 to 7, as said below
- order_second: int32 [32, 8], P('leaf'), may hold values from 0 to 7, as said below
- inverse_third: float32 [128, 128, 128], P('leaf'), may hold values from -0.5 to 0.5
- coupling_third: float32 [128, 3, 128, 128], P('leaf'), may hold values from -0.3125 to 0.3125
- links_third: int32 [128, 3], P('leaf'), may hold values from 0 to 3, as said below
- order_third: int32 [32, 4], P('leaf'), may hold values from 0 to 3, as said below
- front_rows: int32 [3, 32], P(None, 'leaf'), may hold values from 128 to 512
- root_inverse: float32 [2, 8192, 8192], P(None, 'leaf', 'col'), may hold values from -0.0625 to 0.0625
- root_coupling: float32 [8192, 8192], P('leaf', 'col'), may hold values from -0.0625 to 0.0625
Outputs:
- solved_first: float32 [256, 16384], P('col', 'leaf')
- solved_second: float32 [256, 16384], P('col', 'leaf')
- solved_third: float32 [256, 16384], P('col', 'leaf')
- root_solution: float32 [256, 2, 8192], P('col', None, 'leaf')
Inputs may be any that keep to these rules, and one draw needn't show every extreme that they name: `links_first`: each row names 3 different skeleton blocks of its front. `links_second`: each row names 3 different skeleton blocks of its front. `links_third`: each row names 3 different skeleton blocks of its front. `order_first`: each row is a permutation. `order_second`: each row is a permutation. `order_third`: each row is a permutation.
All inputs are finite; a program needn't handle non-finite values.
Results may differ from a plain program's by a relative error of at most 0.0003.
Values sent between devices are 32-bit elements; how exact they have to be, the bound alone decides.
A program may use at most 64 MiB of HBM per device.

v0:
```python
import jax
import jax.numpy as jnp
from jax import lax
from jax.sharding import PartitionSpec as P


def partner(block, axis, stride):
    count = lax.axis_size(axis)
    route = []
    for low in range(count):
        high = low | 1 << stride
        if high != low and high < count:
            route += [(low, high), (high, low)]
    return lax.ppermute(block, axis, route)


def eliminate(section, inverse, coupling, link_ids, live_count):
    block_rows = inverse.shape[-1]
    red_blocks = inverse.shape[0]
    link_total = coupling.shape[1]
    rhs_rows = section.shape[0]
    skeleton_count = section.shape[1] // block_rows - red_blocks
    redundant = section[:, : red_blocks * block_rows].reshape(rhs_rows, red_blocks, block_rows)
    positions = lax.broadcasted_iota(
        jnp.int32, (red_blocks, block_rows), 0
    ) * block_rows + lax.broadcasted_iota(jnp.int32, (red_blocks, block_rows), 1)
    live_rows = (positions < live_count).astype(jnp.float32)
    solved = (
        jnp.einsum("rib,iba->ria", redundant * live_rows, inverse, precision=lax.Precision.HIGHEST)
        * live_rows
    )
    pushed = jnp.einsum("ria,ikab->rikb", solved, coupling, precision=lax.Precision.HIGHEST)
    targets = (
        link_ids[:, :, None]
        == lax.broadcasted_iota(jnp.int32, (red_blocks, link_total, skeleton_count), 2)
    ).astype(jnp.float32)
    update = jnp.einsum("rikb,iks->rsb", pushed, targets, precision=lax.Precision.HIGHEST)
    skeleton = (
        section[:, red_blocks * block_rows :].reshape(rhs_rows, skeleton_count, block_rows) - update
    )
    return (solved.reshape(rhs_rows, red_blocks * block_rows), skeleton)


def join_halves(skeleton, level_index):
    half_blocks = skeleton.shape[1] // 2
    upper_half = lax.axis_index("leaf") >> level_index & 1
    kept_half = lax.dynamic_slice_in_dim(skeleton, upper_half * half_blocks, half_blocks, 1)
    sent_half = lax.dynamic_slice_in_dim(skeleton, (1 - upper_half) * half_blocks, half_blocks, 1)
    received = partner(sent_half, "leaf", level_index)
    return jnp.where(
        upper_half == 0,
        jnp.concatenate([kept_half, received], 1),
        jnp.concatenate([received, kept_half], 1),
    )


def spread_columns(values):
    return lax.all_gather(values, "col", axis=0, tiled=True)


def spread_leaf(values):
    return lax.all_gather(values, "leaf", axis=0, tiled=True)


def to_leaf_rows(values):
    full_rows = lax.all_gather(values, "col", axis=1, tiled=True)
    return lax.all_to_all(full_rows, "leaf", split_axis=1, concat_axis=0, tiled=True)


def to_column_rows(values):
    full_rows = lax.all_gather(values, "leaf", axis=1, tiled=True)
    return lax.all_to_all(full_rows, "col", split_axis=1, concat_axis=0, tiled=True)


def forward_product(values, matrix):
    return lax.psum_scatter(
        jnp.dot(
            values, matrix, precision=lax.Precision.HIGHEST, preferred_element_type=jnp.float32
        ),
        "leaf",
        scatter_dimension=0,
        tiled=True,
    )


def backward_product(values, matrix):
    return lax.psum_scatter(
        lax.dot_general(
            values,
            matrix,
            (((1,), (1,)), ((), ())),
            precision=lax.Precision.HIGHEST,
            preferred_element_type=jnp.float32,
        ),
        "col",
        scatter_dimension=0,
        tiled=True,
    )


def local(
    right_sides,
    inverse_first,
    coupling_first,
    links_first,
    order_first,
    inverse_second,
    coupling_second,
    links_second,
    order_second,
    inverse_third,
    coupling_third,
    links_third,
    order_third,
    front_rows,
    root_inverse,
    root_coupling,
):
    level_data = (
        (inverse_first, coupling_first, links_first, order_first),
        (inverse_second, coupling_second, links_second, order_second),
        (inverse_third, coupling_third, links_third, order_third),
    )
    section = right_sides
    outputs = []
    for level_index in range(3):
        inverse, coupling, link_ids, order_map = level_data[level_index]
        solved, skeleton = eliminate(
            section, inverse, coupling, link_ids, front_rows[level_index, 0]
        )
        outputs.append(solved)
        if level_index < 2:
            skeleton = join_halves(skeleton, level_index)
        skeleton = jnp.take(skeleton, order_map[0], axis=1)
        section = skeleton.reshape(skeleton.shape[0], -1)
    rhs_rows = right_sides.shape[0]
    panel_count = root_inverse.shape[0]
    panel_rows = root_inverse.shape[1]
    root_rhs = section.reshape(rhs_rows, panel_count, panel_rows)
    full_rhs = spread_columns(root_rhs)
    first_solve = forward_product(full_rhs[:, 0], root_inverse[0])
    coupled = forward_product(to_leaf_rows(first_solve), root_coupling)
    second_solve = forward_product(full_rhs[:, 1] - to_leaf_rows(coupled), root_inverse[1])
    forward_both = spread_leaf(jnp.stack([first_solve, second_solve], 1))
    last_panel = backward_product(forward_both[:, 1], root_inverse[1])
    back_coupled = backward_product(to_column_rows(last_panel), root_coupling)
    first_panel = backward_product(
        forward_both[:, 0] - to_column_rows(back_coupled), root_inverse[0]
    )
    root_solution = jnp.stack([first_panel, last_panel], 1)
    return (outputs[0], outputs[1], outputs[2], root_solution)


def solution(mesh):
    in_specs = (
        P("col", "leaf"),
        P("leaf", None, None),
        P("leaf", None, None, None),
        P("leaf", None),
        P("leaf", None),
        P("leaf", None, None),
        P("leaf", None, None, None),
        P("leaf", None),
        P("leaf", None),
        P("leaf", None, None),
        P("leaf", None, None, None),
        P("leaf", None),
        P("leaf", None),
        P(None, "leaf"),
        P(None, "leaf", "col"),
        P("leaf", "col"),
    )
    out_specs = (P("col", "leaf"), P("col", "leaf"), P("col", "leaf"), P("col", None, "leaf"))
    return jax.shard_map(local, mesh=mesh, in_specs=in_specs, out_specs=out_specs, check_vma=False)
```

profile of v0, /device:TPU:1, one launch (start us, length us, event | category | flops | bytes accessed | tf_op | source)
XLA Modules:
  0.0 1211.6 jit_solution(16037484874511490501)
XLA Ops:
  9.6 2.0 fusion.47
  13.9 8.8 collective-permute-start
  29.2 1.9 collective-permute-start.1
  31.3 2.6 collective-permute-done.1
  37.3 52.2 %all_gather.18 = f32[256,2,256]{2,1,0:T(2,128)S(1)} all-gather(f32[16,2,256]{2,1,0:T(2,128)S(1)} %broadcast_select_fusion), channel_id=1, replica_groups=mesh['leaf'=32,'col'=16] {'col'}, dimensions={0}, use_global_device_ids=true | all-gather | bytes 557056 | tf_op jit(solution)/shard_map/all_gather | solution.py:58
  89.7 1.4 fusion.11
  91.2 144.3 %reduce-scatter.7.cloned.1.call-done = f32[8,512]{1,0:T(8,128)} async-done(((f32[256,512]{1,0:T(8,128)}), f32[8,512]{1,0:T(8,128)}) %reduce-scatter.7.cloned.1.call-update) | async-done | bytes 16400 | tf_op jit(solution)/shard_map/reduce_scatter | solution.py:76
  235.5 47.6 %all_gather.19 = f32[8,8192]{1,0:T(8,128)S(1)} all-gather(f32[8,512]{1,0:T(8,128)} %reduce-scatter.7.cloned.1.call-done), channel_id=1, replica_groups=mesh['leaf'=32,'col'=16] {'col'}, dimensions={1}, use_global_device_ids=true | all-gather | bytes 278528 | tf_op jit(solution)/shard_map/all_gather | solution.py:66
  283.1 24.7 %all_to_all.76 = f32[8,32,256]{2,0,1:T(8,128)S(1)} all-to-all(f32[8,32,256]{2,0,1:T(8,128)S(1)} %bitcast.194), channel_id=1, replica_groups=mesh['leaf'=32,'col'=16] {'leaf'}, dimensions={1} | all-to-all | bytes 524288 | tf_op jit(solution)/shard_map/all_to_all | solution.py:67
  307.8 1.4 fusion.21
  309.3 134.3 %reduce-scatter.9.cloned.1.call-done = f32[8,512]{1,0:T(8,128)} async-done(((f32[256,512]{1,0:T(8,128)}), f32[8,512]{1,0:T(8,128)}) %reduce-scatter.9.cloned.1.call-update) | async-done | bytes 16400 | tf_op jit(solution)/shard_map/reduce_scatter | solution.py:76
  443.6 48.0 %all_gather.20 = f32[8,8192]{1,0:T(8,128)S(1)} all-gather(f32[8,512]{1,0:T(8,128)} %reduce-scatter.9.cloned.1.call-done), channel_id=1, replica_groups=mesh['leaf'=32,'col'=16] {'col'}, dimensions={1}, use_global_device_ids=true | all-gather | bytes 278528 | tf_op jit(solution)/shard_map/all_gather | solution.py:66
  491.6 24.2 %all_to_all.77 = f32[8,32,256]{2,0,1:T(8,128)S(1)} all-to-all(f32[8,32,256]{2,0,1:T(8,128)S(1)} %bitcast.192), channel_id=1, replica_groups=mesh['leaf'=32,'col'=16] {'leaf'}, dimensions={1} | all-to-all | bytes 524288 | tf_op jit(solution)/shard_map/all_to_all | solution.py:67
  516.4 1.4 fusion.8
  517.9 134.4 %reduce-scatter.11.cloned.1.call-done = f32[8,512]{1,0:T(8,128)} async-done(((f32[256,512]{1,0:T(8,128)}), f32[8,512]{1,0:T(8,128)}) %reduce-scatter.11.cloned.1.call-update) | async-done | bytes 16400 | tf_op jit(solution)/shard_map/reduce_scatter | solution.py:76
  653.8 66.6 %all-gather.2.cloned.1.call-done = f32[256,2,512]{2,0,1:T(8,128)} async-done(((f32[8,2,512]{2,0,1:T(8,128)}), f32[256,2,512]{2,0,1:T(8,128)}) %all-gather.2.cloned.1.call-update) | async-done | bytes 1048592 | tf_op jit(solution)/shard_map/all_gather | solution.py:62
  720.4 2.4 fusion.3
  722.8 110.5 %reduce-scatter.13.cloned.1.call-done = f32[16,256]{1,0:T(8,128)} async-done(((f32[256,256]{1,0:T(8,128)}), f32[16,256]{1,0:T(8,128)}) %reduce-scatter.13.cloned.1.call-update) | async-done | bytes 16400 | tf_op jit(solution)/shard_map/reduce_scatter | solution.py:87
  833.3 45.5 %all_gather.22 = f32[16,8192]{1,0:T(8,128)S(1)} all-gather(f32[16,256]{1,0:T(8,128)} %reduce-scatter.13.cloned.1.call-done), channel_id=1, replica_groups=mesh['leaf'=32,'col'=16] {'leaf'}, dimensions={1}, use_global_device_ids=true | all-gather | bytes 540672 | tf_op jit(solution)/shard_map/all_gather | solution.py:71
  878.8 35.7 %all_to_all.78 = f32[16,16,512]{2,0,1:T(8,128)S(1)} all-to-all(f32[16,16,512]{2,0,1:T(8,128)S(1)} %bitcast.187), channel_id=1, replica_groups=mesh['leaf'=32,'col'=16] {'col'}, dimensions={1} | all-to-all | bytes 1048576 | tf_op jit(solution)/shard_map/all_to_all | solution.py:72
  915.9 102.4 %reduce-scatter.15.cloned.1.call-done = f32[16,256]{1,0:T(8,128)} async-done(((f32[256,256]{1,0:T(8,128)}), f32[16,256]{1,0:T(8,128)}) %reduce-scatter.15.cloned.1.call-update) | async-done | bytes 16400 | tf_op jit(solution)/shard_map/reduce_scatter | solution.py:87
  1018.3 45.5 %all_gather.23 = f32[16,8192]{1,0:T(8,128)S(1)} all-gather(f32[16,256]{1,0:T(8,128)} %reduce-scatter.15.cloned.1.call-done), channel_id=1, replica_groups=mesh['leaf'=32,'col'=16] {'leaf'}, dimensions={1}, use_global_device_ids=true | all-gather | bytes 540672 | tf_op jit(solution)/shard_map/all_gather | solution.py:71
  1063.8 35.9 %all_to_all.79 = f32[16,16,512]{2,0,1:T(8,128)S(1)} all-to-all(f32[16,16,512]{2,0,1:T(8,128)S(1)} %bitcast.190), channel_id=1, replica_groups=mesh['leaf'=32,'col'=16] {'col'}, dimensions={1} | all-to-all | bytes 1048576 | tf_op jit(solution)/shard_map/all_to_all | solution.py:72
  1102.3 101.1 %reduce-scatter.17.cloned.1.call-done = f32[16,256]{1,0:T(8,128)} async-done(((f32[256,256]{1,0:T(8,128)}), f32[16,256]{1,0:T(8,128)}) %reduce-scatter.17.cloned.1.call-update) | async-done | bytes 16400 | tf_op jit(solution)/shard_map/reduce_scatter | solution.py:87
  (122 shorter events, 22.3 us)
Async XLA Ops:
  7.2 5.7 copy-start
  7.2 228.3 %reduce-scatter.7.cloned.1.call-start = ((), (), s32[]{:S(2)}) async-start(), calls=%async_computation.10 | async-start | bytes 540672 | tf_op jit(solution)/shard_map/reduce_scatter | solution.py:76
  7.2 1.3 copy-start.12
  8.6 0.9 slice-start
  9.5 2.1 copy-start.6
  13.9 8.8 copy-start.15
  13.9 12.4 %collective-permute-start = (f32[16,6,128]{2,1,0:T(8,128)S(1)}, f32[16,6,128]{2,1,0:T(8,128)S(1)}, u32[]{:S(2)}, u32[]{:S(2)}) collective-permute-start(f32[16,6,128]{2,1,0:T(8,128)S(1)} %get-tuple-element.21), channel_id=1, source_target_pairs={{0,16},{16,0},{32,48},{48,32},{64,80},{80,64},{96,112},{112,96},{1... | collective-permute-start | bytes 147464 | tf_op jit(solution)/shard_map/ppermute | solution.py:14
  26.3 1.9 copy-start.4
  27.0 1.0 copy-start.7
  28.3 2.9 copy-start.14
  28.9 6.9 copy-start.5
  29.2 4.7 collective-permute-start.1
  34.5 1.0 copy-start.8
  35.8 53.9 %copy-start.1 = (f32[2,256,512]{2,1,0:T(8,128)S(1)}, f32[2,256,512]{2,1,0:T(8,128)}, u32[]{:S(2)}) copy-start(f32[2,256,512]{2,1,0:T(8,128)} %param.30) | copy-start | bytes 3145732
  91.1 216.7 %copy-start.2 = (f32[256,512]{1,0:T(8,128)S(1)}, f32[256,512]{1,0:T(8,128)}, u32[]{:S(2)}) copy-start(f32[256,512]{1,0:T(8,128)} %param.31) | copy-start | bytes 1572868
  91.1 352.5 %reduce-scatter.9.cloned.1.call-start = ((), (), s32[]{:S(2)}) async-start(), calls=%async_computation.11 | async-start | bytes 540672 | tf_op jit(solution)/shard_map/reduce_scatter | solution.py:76
  309.3 343.1 %reduce-scatter.11.cloned.1.call-start = ((), (), s32[]{:S(2)}) async-start(), calls=%async_computation.12 | async-start | bytes 540672 | tf_op jit(solution)/shard_map/reduce_scatter | solution.py:76
  517.9 134.5 %copy-start.10 = (f32[8,512]{1,0:T(8,128)S(1)}, f32[8,512]{1,0:T(8,128)}, u32[]{:S(2)}) copy-start(f32[8,512]{1,0:T(8,128)} %reduce-scatter.7.cloned.1.call-done) | copy-start | bytes 49156
  517.9 202.5 %all-gather.2.cloned.1.call-start = ((), (), s32[]{:S(2)}) async-start(), calls=%async_computation.13 | async-start | bytes 1081344 | tf_op jit(solution)/shard_map/all_gather | solution.py:62
  653.7 179.5 %reduce-scatter.13.cloned.1.call-start = ((), (), s32[]{:S(2)}) async-start(), calls=%async_computation.14 | async-start | bytes 278528 | tf_op jit(solution)/shard_map/reduce_scatter | solution.py:87
  722.7 295.5 %reduce-scatter.15.cloned.1.call-start = ((), (), s32[]{:S(2)}) async-start(), calls=%async_computation.15 | async-start | bytes 278528 | tf_op jit(solution)/shard_map/reduce_scatter | solution.py:87
  915.8 287.5 %reduce-scatter.17.cloned.1.call-start = ((), (), s32[]{:S(2)}) async-start(), calls=%async_computation.16 | async-start | bytes 278528 | tf_op jit(solution)/shard_map/reduce_scatter | solution.py:87
  1063.7 35.9 %copy-start.3 = (f32[256,2,512]{2,0,1:T(8,128)S(1)}, f32[256,2,512]{2,0,1:T(8,128)}, u32[]{:S(2)}) copy-start(f32[256,2,512]{2,0,1:T(8,128)} %all-gather.2.cloned.1.call-done) | copy-start | bytes 3145732
  1101.6 101.7 %copy-start.9 = (f32[16,256]{1,0:T(8,128)S(1)}, f32[16,256]{1,0:T(8,128)}, u32[]{:S(2)}) copy-start(f32[16,256]{1,0:T(8,128)} %reduce-scatter.13.cloned.1.call-done) | copy-start | bytes 49156
  (4 other events, 2.7 us)
Sparse Core Ops, SparseCore 0:
  91.2 144.2 reduce-scatter.6
  309.4 134.1 reduce-scatter.8
  518.0 134.3 reduce-scatter.10
  655.2 65.1 all-gather.1
  724.8 108.4 reduce-scatter.12
  915.9 102.3 reduce-scatter.14
  1101.1 102.1 reduce-scatter.16
where the time goes:
time: 1210 us
  waiting for transfers between devices  796 us (66%)
  blocking collectives  359 us (30%)
  between operations  14.6 us (1%)
  matrix products  13.9 us (1%)
    reduce_scatter x3, waiting for transfers between devices, forward_product(): lax.psum_scatter(jnp.dot(values, matrix, precision=lax.Precision.HIGHEST,...  413 us
    reduce_scatter x3, waiting for transfers between devices, backward_product(): lax.psum_scatter(lax.dot_general(values, matrix, (((1,), (1,)), ((), ()))...  314 us
    all_gather x2, blocking collectives, to_leaf_rows(): full_rows = lax.all_gather(values, 'col', axis=1, tiled=True)  95.6 us
    all_gather x2, blocking collectives, to_column_rows(): full_rows = lax.all_gather(values, 'leaf', axis=1, tiled=True)  90.9 us
    all_to_all x2, blocking collectives, to_column_rows(): lax.all_to_all(full_rows, 'col', split_axis=1, concat_axis=0, tiled=True)  71.5 us
    all_gather x1, waiting for transfers between devices, spread_leaf(): return lax.all_gather(values, 'leaf', axis=0, tiled=True)  66.6 us
    all_gather x1, blocking collectives, spread_columns(): return lax.all_gather(values, 'col', axis=0, tiled=True)  52.2 us
    all_to_all x2, blocking collectives, to_leaf_rows(): lax.all_to_all(full_rows, 'leaf', split_axis=1, concat_axis=0, tiled=True)  48.9 us
  transfers between devices with their start and end apart: 9, of which 8 were waited for; matrix products, arithmetic and copies ran while one was open for 0% of the time, Pallas kernels for 0%

commit v1 on v0

--- a/solution.py
+++ b/solution.py
@@ -1,7 +1,19 @@
 import jax
 import jax.numpy as jnp
 from jax import lax
+from jax.experimental import pallas as pl
+from jax.experimental.pallas import tpu as pltpu
 from jax.sharding import PartitionSpec as P
+
+MESH = pl.DeviceIdType.MESH
+SIDE = 4
+ROWS = 8
+GROUPS = SIDE * SIDE
+TOTAL = GROUPS * ROWS
+HALF = 256
+SPAN = 512
+STEPS = 6
+MESSAGES = 96
 
 
 def partner(block, axis, stride):
@@ -54,48 +66,323 @@
     )
 
 
-def spread_columns(values):
-    return lax.all_gather(values, "col", axis=0, tiled=True)
-
-
-def spread_leaf(values):
-    return lax.all_gather(values, "leaf", axis=0, tiled=True)
-
-
-def to_leaf_rows(values):
-    full_rows = lax.all_gather(values, "col", axis=1, tiled=True)
-    return lax.all_to_all(full_rows, "leaf", split_axis=1, concat_axis=0, tiled=True)
-
-
-def to_column_rows(values):
-    full_rows = lax.all_gather(values, "leaf", axis=1, tiled=True)
-    return lax.all_to_all(full_rows, "col", split_axis=1, concat_axis=0, tiled=True)
-
-
-def forward_product(values, matrix):
-    return lax.psum_scatter(
-        jnp.dot(
-            values, matrix, precision=lax.Precision.HIGHEST, preferred_element_type=jnp.float32
+def device(x, z_lo, core, y, z_hi):
+    return (x * (2 * SIDE) + z_lo * 2 + core, y * SIDE + z_hi)
+
+
+def root_kernel(
+    section,
+    inverse,
+    coupling,
+    out,
+    own,
+    sibling,
+    high,
+    low,
+    pieces,
+    turned,
+    gathered,
+    partial,
+    first_in,
+    first_sum,
+    second_in,
+    solved,
+    final_in,
+    send_sem,
+    recv_sem,
+    local_sem,
+):
+    leaf, col = lax.axis_index("leaf"), lax.axis_index("col")
+    x, z_lo, core = leaf // (2 * SIDE), leaf // 2 % SIDE, leaf % 2
+    y, z_hi = col // SIDE, col % SIDE
+    chip_row = leaf // 2
+    other = 1 - core
+    same = jnp.logical_and(x == y, z_lo == z_hi)
+
+    def around(axis, step):
+        at = {"x": x, "z_lo": z_lo, "y": y, "z_hi": z_hi}
+        at[axis] = lax.rem(at[axis] + step, SIDE)
+        return device(at["x"], at["z_lo"], core, at["y"], at["z_hi"])
+
+    twin = device(x, z_lo, other, y, z_hi)
+    turn_forward = [device(y, z_hi, core, x, k) for k in range(SIDE)]
+    turn_backward = [device(y, k, core, x, z_lo) for k in range(SIDE)]
+
+    barrier = pltpu.get_barrier_semaphore()
+    pl.semaphore_signal(barrier, inc=1, device_id=twin, device_id_type=MESH)
+    for axis in ("x", "z_lo", "y", "z_hi"):
+        for step in range(1, SIDE):
+            pl.semaphore_signal(barrier, inc=1, device_id=around(axis, step), device_id_type=MESH)
+    for targets, mine in ((turn_forward, z_hi), (turn_backward, z_lo)):
+        for k in range(SIDE):
+            itself = jnp.logical_and(same, mine == k)
+
+            @pl.when(jnp.logical_not(itself))
+            def _():
+                pl.semaphore_signal(barrier, inc=1, device_id=targets[k], device_id_type=MESH)
+
+    loads = []
+    for k in range(3):
+        source = coupling if k == 1 else inverse.at[k // 2]
+        loads.append(pltpu.make_async_copy(source, own.at[k], local_sem.at[k]))
+        loads[-1].start()
+    pl.semaphore_wait(barrier, 1 + 4 * (SIDE - 1) + 2 * SIDE - 2 * same.astype(jnp.int32))
+
+    used = [0]
+    pending = []
+
+    def take(count):
+        used[0] += count
+        return used[0] - count
+
+    def send(source, target, to):
+        n = take(1)
+        copy = pltpu.make_async_remote_copy(
+            src_ref=source,
+            dst_ref=target,
+            send_sem=send_sem.at[n],
+            recv_sem=recv_sem.at[n],
+            device_id=to,
+            device_id_type=MESH,
+        )
+        copy.start()
+        pending.append(copy.wait_send)
+        return copy
+
+    def send_unless_same(source, target, to, itself, sent, received):
+        remote = pltpu.make_async_remote_copy(
+            src_ref=source,
+            dst_ref=target,
+            send_sem=send_sem.at[sent],
+            recv_sem=recv_sem.at[received],
+            device_id=to,
+            device_id_type=MESH,
+        )
+
+        @pl.when(jnp.logical_not(itself))
+        def _():
+            remote.start()
+
+        @pl.when(itself)
+        def _():
+            pltpu.make_async_copy(source, target, recv_sem.at[received]).start()
+
+        def finish():
+            @pl.when(jnp.logical_not(itself))
+            def _():
+                remote.wait_send()
+
+        pending.append(finish)
+        return remote
+
+    mine_at = pl.multiple_of(core * HALF, HALF)
+    other_at = pl.multiple_of(other * HALF, HALF)
+    kept = pl.ds(pl.multiple_of(core * ROWS, ROWS), ROWS)
+    given = pl.ds(pl.multiple_of(other * ROWS, ROWS), ROWS)
+    swaps = [
+        send(
+            section.at[given, pl.ds(p * HALF, HALF)],
+            pieces.at[p, :, pl.ds(mine_at, HALF)],
+            twin,
+        )
+        for p in range(2)
+    ]
+    factors = [
+        send(coupling if k == 1 else inverse.at[k // 2], sibling.at[k], twin) for k in range(3)
+    ]
+    for p in range(2):
+        pieces[p, :, pl.ds(mine_at, HALF)] = section[kept, p * HALF : (p + 1) * HALF]
+
+    def rows_of(group):
+        return pl.ds(pl.multiple_of(group * ROWS, ROWS), ROWS)
+
+    def band_of(member):
+        return pl.ds(pl.multiple_of(member * SIDE * ROWS, SIDE * ROWS), SIDE * ROWS)
+
+    def gather_second(step, axis, member):
+        band = gathered.at[step, band_of(member)]
+        copies = [send(band, band, around(axis, d)) for d in (2, 1, 3)]
+        return copies
+
+    def gather_plain(step, piece, group, near, far, member):
+        target = gathered.at[step, rows_of(group)]
+        copies = [send(piece, target, around(near, d)) for d in (2, 1, 3)]
+        gathered[step, rows_of(group)] = piece[...]
+        for copy in copies:
+            copy.wait_recv()
+        return gather_second(step, far, member)
+
+    def gather_turned(step, piece, group, targets, mine, slot, far, member):
+        target = gathered.at[step, rows_of(group)]
+        base = take(SIDE)
+        for k in range(SIDE):
+            send_unless_same(
+                piece,
+                target,
+                targets[k],
+                jnp.logical_and(same, mine == k),
+                base + k,
+                base + slot,
+            )
+        for k in range(SIDE):
+            pltpu.make_async_remote_copy(
+                src_ref=piece,
+                dst_ref=target,
+                send_sem=send_sem.at[base + k],
+                recv_sem=recv_sem.at[base + k],
+                device_id=twin,
+                device_id_type=MESH,
+            ).wait_recv()
+        return gather_second(step, far, member)
+
+    def split(k):
+        for source, at in ((own, mine_at), (sibling, other_at)):
+            if source is own:
+                loads[k].wait()
+            else:
+                factors[k].wait_recv()
+            value = source[k]
+            top = value.astype(jnp.bfloat16)
+            high[k, pl.ds(at, HALF), :] = top
+            low[k, pl.ds(at, HALF), :] = (value - top.astype(jnp.float32)).astype(jnp.bfloat16)
+
+    def multiply(step, k, transposed):
+        value = gathered[step]
+        top = value.astype(jnp.bfloat16)
+        rest = (value - top.astype(jnp.float32)).astype(jnp.bfloat16)
+        both = jnp.concatenate([top, rest], 0)
+        for half in range(2):
+            cut = slice(half * HALF, (half + 1) * HALF)
+            if transposed:
+                right_high, right_low = high[k, cut, :], low[k, cut, :]
+            else:
+                right_high, right_low = high[k, :, cut], low[k, :, cut]
+            dims = (((1,), (1 if transposed else 0,)), ((), ()))
+            wide = lax.dot_general(both, right_high, dims, preferred_element_type=jnp.float32)
+            thin = lax.dot_general(top, right_low, dims, preferred_element_type=jnp.float32)
+            partial[step, :, cut] = wide[:TOTAL] + (wide[TOTAL:] + thin)
+
+    def reduce(step, far, near, far_at, near_at, meanwhile=None):
+        copies = []
+        for d in (2, 1, 3):
+            to = lax.rem(far_at + d, SIDE)
+            copies.append(
+                send(partial.at[step, band_of(to)], first_in.at[step, d - 1], around(far, d))
+            )
+        if meanwhile is not None:
+            meanwhile()
+        for copy in copies:
+            copy.wait_recv()
+        total = partial[step, band_of(far_at)]
+        first_sum[step] = total + first_in[step, 0] + (first_in[step, 1] + first_in[step, 2])
+        copies = []
+        for d in (2, 1, 3):
+            to = lax.rem(near_at + d, SIDE)
+            copies.append(
+                send(first_sum.at[step, rows_of(to)], second_in.at[step, d - 1], around(near, d))
+            )
+        for copy in copies:
+            copy.wait_recv()
+        total = first_sum[step, rows_of(near_at)]
+        return total + second_in[step, 0] + (second_in[step, 1] + second_in[step, 2])
+
+    def wait_all(copies):
+        for copy in copies:
+            copy.wait_recv()
+
+    def give_result(step, panel):
+        copy = send(
+            solved.at[step, :, pl.ds(other_at, HALF)], final_in.at[panel], twin
+        )
+        out[kept, panel * HALF : (panel + 1) * HALF] = solved[step, :, pl.ds(mine_at, HALF)]
+        return copy
+
+    def take_result(copy, panel):
+        copy.wait_recv()
+        out[given, panel * HALF : (panel + 1) * HALF] = final_in[panel]
+
+    swaps[0].wait_recv()
+    copies = gather_plain(0, pieces.at[0], col, "z_hi", "y", y)
+    swaps[1].wait_recv()
+    n = take(1)
+    turning = send_unless_same(
+        pieces.at[1], turned, device(y, z_hi, core, x, z_lo), same, n, n
+    )
+    split(0)
+    wait_all(copies)
+
+    multiply(0, 0, False)
+    solved[0] = reduce(0, "x", "z_lo", x, z_lo, lambda: split(1))
+    copies = gather_turned(1, solved.at[0], chip_row, turn_forward, z_hi, z_lo, "y", y)
+    wait_all(copies)
+
+    multiply(1, 1, False)
+    total = reduce(1, "x", "z_lo", x, z_lo, lambda: split(2))
+    turning.wait_recv()
+    solved[1] = turned[...] - total
+    copies = gather_turned(2, solved.at[1], chip_row, turn_forward, z_hi, z_lo, "y", y)
+    wait_all(copies)
+
+    multiply(2, 2, False)
+    solved[2] = reduce(2, "x", "z_lo", x, z_lo)
+    copies = gather_plain(3, solved.at[2], chip_row, "z_lo", "x", x)
+    wait_all(copies)
+
+    multiply(3, 2, True)
+    solved[3] = reduce(3, "y", "z_hi", y, z_hi)
+    copies = gather_turned(4, solved.at[3], col, turn_backward, z_lo, z_hi, "x", x)
+    last = give_result(3, 1)
+    wait_all(copies)
+
+    multiply(4, 1, True)
+    total = reduce(4, "y", "z_hi", y, z_hi)
+    solved[4] = gathered[1, rows_of(col)] - total
+    copies = gather_turned(5, solved.at[4], col, turn_backward, z_lo, z_hi, "x", x)
+    wait_all(copies)
+
+    multiply(5, 0, True)
+    solved[5] = reduce(5, "y", "z_hi", y, z_hi)
+    first = give_result(5, 0)
+    take_result(last, 1)
+    take_result(first, 0)
+    for finish in pending:
+        finish()
+
+
+def root_solve(section, root_inverse, root_coupling):
+    f32, bf16 = jnp.float32, jnp.bfloat16
+    return pl.pallas_call(
+        root_kernel,
+        out_shape=jax.ShapeDtypeStruct((2 * ROWS, 2 * HALF), f32),
+        in_specs=[
+            pl.BlockSpec(memory_space=pltpu.VMEM),
+            pl.BlockSpec(memory_space=pl.ANY),
+            pl.BlockSpec(memory_space=pl.ANY),
+        ],
+        out_specs=pl.BlockSpec(memory_space=pltpu.VMEM),
+        scratch_shapes=[
+            pltpu.VMEM((3, HALF, SPAN), f32),
+            pltpu.VMEM((3, HALF, SPAN), f32),
+            pltpu.VMEM((3, SPAN, SPAN), bf16),
+            pltpu.VMEM((3, SPAN, SPAN), bf16),
+            pltpu.VMEM((2, ROWS, SPAN), f32),
+            pltpu.VMEM((ROWS, SPAN), f32),
+            pltpu.VMEM((STEPS, TOTAL, SPAN), f32),
+            pltpu.VMEM((STEPS, TOTAL, SPAN), f32),
+            pltpu.VMEM((STEPS, SIDE - 1, SIDE * ROWS, SPAN), f32),
+            pltpu.VMEM((STEPS, SIDE * ROWS, SPAN), f32),
+            pltpu.VMEM((STEPS, SIDE - 1, ROWS, SPAN), f32),
+            pltpu.VMEM((STEPS, ROWS, SPAN), f32),
+            pltpu.VMEM((2, ROWS, HALF), f32),
+            pltpu.SemaphoreType.DMA((MESSAGES,)),
+            pltpu.SemaphoreType.DMA((MESSAGES,)),
+            pltpu.SemaphoreType.DMA((3,)),
+        ],
+        compiler_params=pltpu.CompilerParams(
+            collective_id=0, has_side_effects=True, vmem_limit_bytes=40 << 20
         ),
-        "leaf",
-        scatter_dimension=0,
-        tiled=True,
-    )
-
-
-def backward_product(values, matrix):
-    return lax.psum_scatter(
-        lax.dot_general(
-            values,
-            matrix,
-            (((1,), (1,)), ((), ())),
-            precision=lax.Precision.HIGHEST,
-            preferred_element_type=jnp.float32,
-        ),
-        "col",
-        scatter_dimension=0,
-        tiled=True,
-    )
+        name="root_solve",
+    )(section, root_inverse, root_coupling)
 
 
 def local(
@@ -133,22 +420,9 @@
             skeleton = join_halves(skeleton, level_index)
         skeleton = jnp.take(skeleton, order_map[0], axis=1)
         section = skeleton.reshape(skeleton.shape[0], -1)
+    root_solution = root_solve(section, root_inverse, root_coupling)
     rhs_rows = right_sides.shape[0]
-    panel_count = root_inverse.shape[0]
-    panel_rows = root_inverse.shape[1]
-    root_rhs = section.reshape(rhs_rows, panel_count, panel_rows)
-    full_rhs = spread_columns(root_rhs)
-    first_solve = forward_product(full_rhs[:, 0], root_inverse[0])
-    coupled = forward_product(to_leaf_rows(first_solve), root_coupling)
-    second_solve = forward_product(full_rhs[:, 1] - to_leaf_rows(coupled), root_inverse[1])
-    forward_both = spread_leaf(jnp.stack([first_solve, second_solve], 1))
-    last_panel = backward_product(forward_both[:, 1], root_inverse[1])
-    back_coupled = backward_product(to_column_rows(last_panel), root_coupling)
-    first_panel = backward_product(
-        forward_both[:, 0] - to_column_rows(back_coupled), root_inverse[0]
-    )
-    root_solution = jnp.stack([first_panel, last_panel], 1)
-    return (outputs[0], outputs[1], outputs[2], root_solution)
+    return (*outputs, root_solution.reshape(rhs_rows, 2, HALF))
 
 
 def solution(mesh):

time: 1210 us -> 190 us (0.16)
  waiting for transfers between devices: 796 us -> 2.61 us
  blocking collectives: 359 us -> 0 us
  Pallas kernels: 0 us -> 158 us
  between operations: 14.6 us -> 1.04 us
    reduce_scatter x6 -> x0, waiting for transfers between devices: 727 us -> none  [the longest x3 413 us: forward_product(): lax.psum_scatter(jnp.dot(values, matrix, precision=lax.Precision.HIGHEST,...]
    all_gather x5 -> x0, blocking collectives: 239 us -> none  [the longest x2 95.6 us: to_leaf_rows(): full_rows = lax.all_gather(values, 'col', axis=1, tiled=True)]
    pallas_call x0 -> x1, Pallas kernels: none -> 158 us  [root_solve(): pl.pallas_call(root_kernel, out_shape=jax.ShapeDtypeStruct((2 * ROWS, 2 *...]
    all_to_all x4 -> x0, blocking collectives: 120 us -> none  [the longest x2 71.5 us: to_column_rows(): lax.all_to_all(full_rows, 'col', split_axis=1, concat_axis=0, tiled=True)]
    all_gather x1 -> x0, waiting for transfers between devices: 66.6 us -> none  [spread_leaf(): return lax.all_gather(values, 'leaf', axis=0, tiled=True)]
  transfers between devices with their start and end apart: 9 -> 2, of which waited for: 8 -> 1; matrix products, arithmetic and copies ran while one was open for 0% -> 1% of each run, Pallas kernels for 0% -> 0%
where the time goes in v1:
time: 190 us; the launch traced here: 189 us
  Pallas kernels  158 us (83%)
  starting transfers between devices  10.8 us (6%)
  local copies, waits for them, and re-layouts  9.98 us (5%)
  matrix products  4.6 us (2%)
  waiting for transfers between devices  2.61 us (1%)
  other arithmetic  2.17 us (1%)
    pallas_call x1, Pallas kernels, root_solve(): pl.pallas_call(root_kernel, out_shape=jax.ShapeDtypeStruct((2 * ROWS, 2 *...  158 us
    ppermute x2, starting transfers between devices, partner(): return lax.ppermute(block, axis, route)  10.8 us
    unnamed x37, local copies, waits for them, and re-layouts  4.54 us
  transfers between devices with their start and end apart: 2, of which 1 were waited for; matrix products, arithmetic and copies ran while one was open for 1% of the time, Pallas kernels for 0%

profile of v1, /device:TPU:1, one launch (start us, length us, event | category | flops | bytes accessed | tf_op | source)
XLA Modules:
  0.0 189.2 jit_solution(16547437341514846357)
XLA Ops:
  0.7 0.7 copy-done.8
  1.4 0.6 fusion.32
  2.0 0.9 slice-done
  2.9 0.7 copy-done.9
  3.6 2.0 %fusion.27 = (f32[4,128]{1,0:T(4,128)S(1)}, f32[4,128]{1,0:T(4,128)S(1)}, f32[4,128]{1,0:T(4,128)S(1)}) fusion(s32[]{:T(128)} %bitcast.28, s32[4]{0:T(128)S(1)} %iota_multiply_fusion, s32[]{:T(128)} %bitcast.14, s32[]{:T(128)} %bitcast), kind=kLoop, calls=%fused_computation.63 | loop fusion | flops 3584 | bytes 6172 | tf_op jit(solution)/shard_map/convert_element_type | solution.py:39
  5.7 1.3 convolution_multiply_fusion.2
  6.9 0.6 convolution_bitcast_fusion.3
  7.5 0.3 fusion
  7.9 8.8 %collective-permute-start = (f32[16,6,128]{2,1,0:T(8,128)S(1)}, f32[16,6,128]{2,1,0:T(8,128)S(1)}, u32[]{:S(2)}, u32[]{:S(2)}) collective-permute-start(f32[16,6,128]{2,1,0:T(8,128)S(1)} %get-tuple-element.5), channel_id=1, source_target_pairs={{0,16},{16,0},{32,48},{48,32},{64,80},{80,64},{96,112},{112,96},{1... | collective-permute-start | bytes 147464 | tf_op jit(solution)/shard_map/ppermute | solution.py:26
  16.7 0.6 copy_bitcast_fusion.2
  17.4 0.6 copy-done.13
  18.0 0.6 copy-done.14
  18.9 0.7 copy-done.10
  19.8 0.6 gather_fusion
  20.5 0.8 copy-done.6
  21.7 0.6 convolution_bitcast_fusion.2
  22.6 2.1 %collective-permute-start.1 = (f32[16,4,128]{2,1,0:T(4,128)S(1)}, f32[16,4,128]{2,1,0:T(4,128)S(1)}, u32[]{:S(2)}, u32[]{:S(2)}) collective-permute-start(f32[16,4,128]{2,1,0:T(4,128)S(1)} %get-tuple-element.9), channel_id=1, source_target_pairs={{0,32},{32,0},{16,48},{48,16},{64,96},{96,64},{80,112},{112,80},{1... | collective-permute-start | bytes 98312 | tf_op jit(solution)/shard_map/ppermute | solution.py:26
  24.8 2.6 %collective-permute-done.1 = f32[16,4,128]{2,1,0:T(4,128)S(1)} collective-permute-done((f32[16,4,128]{2,1,0:T(4,128)S(1)}, f32[16,4,128]{2,1,0:T(4,128)S(1)}, u32[]{:S(2)}, u32[]{:S(2)}) %collective-permute-start.1) | collective-permute-done | bytes 32800 | tf_op jit(solution)/shard_map/ppermute | solution.py:26
  27.5 0.6 gather_fusion.1
  28.5 0.6 copy_bitcast_fusion
  29.1 0.6 convolution_bitcast_fusion.1
  30.0 0.6 gather_fusion.2
  30.6 158.0 %root_solve.1 = f32[16,512]{1,0:T(8,128)S(1)} custom-call(f32[16,512]{1,0:T(8,128)S(1)} %bitcast_select_fusion.2.section, f32[2,256,512]{2,1,0:T(8,128)S(1)} %copy-done.1, f32[256,512]{1,0:T(8,128)S(1)} %copy-done.2), custom_call_target="tpu_custom_call" | custom-call | tf_op jit(solution)/shard_map/root_solve/pallas_call | solution.py:354
  188.6 0.6 reshape.202
  (68 shorter events, 2.2 us)
Async XLA Ops:
  0.6 6.3 %copy-start = (f32[4,3,128,128]{3,2,1,0:T(8,128)S(1)}, f32[4,3,128,128]{3,2,1,0:T(8,128)}, u32[]{:S(2)}) copy-start(f32[4,3,128,128]{3,2,1,0:T(8,128)} %param.18) | copy-start | bytes 2359300
  0.7 0.7 copy-start.8
  2.0 0.9 slice-start
  2.9 0.7 copy-start.9
  2.9 2.8 %copy-start.5 = (f32[16,2048]{1,0:T(8,128)S(1)}, f32[16,2048]{1,0:T(8,128)}, u32[]{:S(2)}) copy-start(f32[16,2048]{1,0:T(8,128)} %param.16) | copy-start | bytes 393220
  7.9 9.4 %copy-start.12 = (s32[1,12]{1,0:T(1,128)S(1)}, s32[1,12]{1,0:T(1,128)}, u32[]{:S(2)}) copy-start(s32[1,12]{1,0:T(1,128)} %param.20) | copy-start | bytes 148
  7.9 11.8 %collective-permute-start = (f32[16,6,128]{2,1,0:T(8,128)S(1)}, f32[16,6,128]{2,1,0:T(8,128)S(1)}, u32[]{:S(2)}, u32[]{:S(2)}) collective-permute-start(f32[16,6,128]{2,1,0:T(8,128)S(1)} %get-tuple-element.5), channel_id=1, source_target_pairs={{0,16},{16,0},{32,48},{48,32},{64,80},{80,64},{96,112},{112,96},{1... | collective-permute-start | bytes 147464 | tf_op jit(solution)/shard_map/ppermute | solution.py:26
  17.3 0.7 copy-start.13
  18.0 0.7 copy-start.14
  18.9 0.7 copy-start.10
  19.7 1.9 %copy-start.3 = (f32[4,3,128,128]{3,2,1,0:T(8,128)S(1)}, f32[4,3,128,128]{3,2,1,0:T(8,128)}, u32[]{:S(2)}) copy-start(f32[4,3,128,128]{3,2,1,0:T(8,128)} %param.22) | copy-start | bytes 2359300
  20.4 1.0 copy-start.6
  22.2 2.5 %copy-start.11 = (s32[4,3]{1,0:T(4,128)S(1)}, s32[4,3]{1,0:T(4,128)}, u32[]{:S(2)}) copy-start(s32[4,3]{1,0:T(4,128)} %param.27) | copy-start | bytes 148
  22.2 5.9 %copy-start.7 = (f32[4,128,128]{2,1,0:T(8,128)S(1)}, f32[4,128,128]{2,1,0:T(8,128)}, u32[]{:S(2)}) copy-start(f32[4,128,128]{2,1,0:T(8,128)} %param.25) | copy-start | bytes 786436
  22.6 6.5 %copy-start.4 = (f32[4,3,128,128]{3,2,1,0:T(8,128)S(1)}, f32[4,3,128,128]{3,2,1,0:T(8,128)}, u32[]{:S(2)}) copy-start(f32[4,3,128,128]{3,2,1,0:T(8,128)} %param.26) | copy-start | bytes 2359300
  22.6 4.8 %collective-permute-start.1 = (f32[16,4,128]{2,1,0:T(4,128)S(1)}, f32[16,4,128]{2,1,0:T(4,128)S(1)}, u32[]{:S(2)}, u32[]{:S(2)}) collective-permute-start(f32[16,4,128]{2,1,0:T(4,128)S(1)} %get-tuple-element.9), channel_id=1, source_target_pairs={{0,32},{32,0},{16,48},{48,16},{64,96},{96,64},{80,112},{112,80},{1... | collective-permute-start | bytes 98312 | tf_op jit(solution)/shard_map/ppermute | solution.py:26
  28.0 2.5 %copy-start.1 = (f32[2,256,512]{2,1,0:T(8,128)S(1)}, f32[2,256,512]{2,1,0:T(8,128)}, u32[]{:S(2)}) copy-start(f32[2,256,512]{2,1,0:T(8,128)} %inverse.1) | copy-start | bytes 3145732
  29.1 1.5 copy-start.2

commit v2 on v1

v2 whole, which is shorter than its diff:
```python
import jax
import jax.numpy as jnp
from jax import lax
from jax.experimental import pallas as pl
from jax.experimental.pallas import tpu as pltpu
from jax.sharding import PartitionSpec as P

MESH = pl.DeviceIdType.MESH
SIDE = 4
ROWS = 8
GROUPS = SIDE * SIDE
TOTAL = GROUPS * ROWS
HALF = 256
SPAN = 512
BLOCK = 128
RED = 4
LINKS = 3
SKELETONS = (12, 8, 4)
STEPS = 6
MESSAGES = 160


def device(x, z_lo, core, y, z_hi):
    return (x * (2 * SIDE) + z_lo * 2 + core, y * SIDE + z_hi)


def rows_of(group):
    return pl.ds(pl.multiple_of(group * ROWS, ROWS), ROWS)


def band_of(member):
    return pl.ds(pl.multiple_of(member * SIDE * ROWS, SIDE * ROWS), SIDE * ROWS)


def solve_kernel(
    right_sides,
    inverse_first,
    coupling_first,
    links_first,
    order_first,
    inverse_second,
    coupling_second,
    links_second,
    order_second,
    inverse_third,
    coupling_third,
    links_third,
    order_third,
    front_rows,
    root_inverse,
    root_coupling,
    out_first,
    out_second,
    out_third,
    out,
    first_rows,
    front_inverse,
    front_coupling,
    front_solve,
    front_push,
    updated,
    joined_first,
    joined_second,
    joined_third,
    section,
    own,
    sibling,
    high,
    low,
    pieces,
    turned,
    crossed,
    moved,
    gathered,
    partial,
    leaf_in,
    first_in,
    first_sum,
    second_in,
    quarter,
    solved,
    final_in,
    send_sem,
    recv_sem,
    local_sem,
):
    leaf, col = lax.axis_index("leaf"), lax.axis_index("col")
    x, z_lo, core = leaf // (2 * SIDE), leaf // 2 % SIDE, leaf % 2
    y, z_hi = col // SIDE, col % SIDE
    chip_row = leaf // 2
    other = 1 - core
    same_plane = x == y
    same_depth = z_lo == z_hi

    def around(axis, step):
        at = {"x": x, "z_lo": z_lo, "y": y, "z_hi": z_hi}
        at[axis] = lax.rem(at[axis] + step, SIDE)
        return device(at["x"], at["z_lo"], core, at["y"], at["z_hi"])

    twin = device(x, z_lo, other, y, z_hi)
    neighbour = device(x, z_lo + 1 - 2 * (z_lo % 2), core, y, z_hi)
    sunk = device(x, z_hi, core, y, z_lo)
    flipped = device(y, z_lo, core, x, z_hi)
    leaf_steps = [(a, b) for a in (2, 1, 3, 0) for b in (3, 2, 1, 0) if a or b]
    leaf_targets = [
        device(lax.rem(x + a, SIDE), lax.rem(z_lo + b, SIDE), core, y, z_hi) for a, b in leaf_steps
    ]
    depth_forward = (
        [device(x, z_hi, core, y, k) for k in range(SIDE)],
        [jnp.logical_and(same_depth, z_hi == k) for k in range(SIDE)],
        z_lo,
    )
    depth_backward = (
        [device(x, k, core, y, z_lo) for k in range(SIDE)],
        [jnp.logical_and(same_depth, z_lo == k) for k in range(SIDE)],
        z_hi,
    )
    plane_forward = (
        [device(y, z_lo, core, k, z_hi) for k in range(SIDE)],
        [jnp.logical_and(same_plane, y == k) for k in range(SIDE)],
        x,
    )
    plane_backward = (
        [device(k, z_lo, core, x, z_hi) for k in range(SIDE)],
        [jnp.logical_and(same_plane, x == k) for k in range(SIDE)],
        y,
    )

    front_data = (
        (inverse_first, coupling_first, links_first, order_first, out_first),
        (inverse_second, coupling_second, links_second, order_second, out_second),
        (inverse_third, coupling_third, links_third, order_third, out_third),
    )
    first_load = pltpu.make_async_copy(right_sides, first_rows, local_sem.at[9])
    first_load.start()
    front_loads = []
    for level in range(3):
        pair = (
            pltpu.make_async_copy(
                front_data[level][0], front_inverse.at[level], local_sem.at[2 * level]
            ),
            pltpu.make_async_copy(
                front_data[level][1], front_coupling.at[level], local_sem.at[2 * level + 1]
            ),
        )
        for load in pair:
            load.start()
        front_loads.append(pair)
    factor_of = (root_inverse.at[0], root_coupling, root_inverse.at[1])
    loads = []
    for k in range(3):
        loads.append(pltpu.make_async_copy(factor_of[k], own.at[k], local_sem.at[6 + k]))
        loads[-1].start()

    barrier = pltpu.get_barrier_semaphore()

    def greet(to):
        pl.semaphore_signal(barrier, inc=1, device_id=to, device_id_type=MESH)

    greet(twin)
    for to in leaf_targets:
        greet(to)
    for axis in ("y", "z_hi"):
        for step in range(1, SIDE):
            greet(around(axis, step))
    for targets, itself, _ in (depth_forward, depth_backward, plane_forward, plane_backward):
        for k in range(SIDE):

            @pl.when(jnp.logical_not(itself[k]))
            def _():
                greet(targets[k])

    used = [0]
    pending = []

    def take(count):
        used[0] += count
        return used[0] - count

    def send(source, target, to):
        n = take(1)
        copy = pltpu.make_async_remote_copy(
            src_ref=source,
            dst_ref=target,
            send_sem=send_sem.at[n],
            recv_sem=recv_sem.at[n],
            device_id=to,
            device_id_type=MESH,
        )
        copy.start()
        pending.append(copy.wait_send)
        return copy

    def send_unless_same(source, target, to, itself, sent, received):
        remote = pltpu.make_async_remote_copy(
            src_ref=source,
            dst_ref=target,
            send_sem=send_sem.at[sent],
            recv_sem=recv_sem.at[received],
            device_id=to,
            device_id_type=MESH,
        )

        @pl.when(jnp.logical_not(itself))
        def _():
            remote.start()

        @pl.when(itself)
        def _():
            pltpu.make_async_copy(source, target, recv_sem.at[received]).start()

        def finish():
            @pl.when(jnp.logical_not(itself))
            def _():
                remote.wait_send()

        pending.append(finish)
        return remote

    def flush(count):
        for finish in pending[:count]:
            finish()
        del pending[:count]

    def wait_all(copies):
        for copy in copies:
            copy.wait_recv()

    def turn(source, target, route):
        targets, itself, slot = route
        base = take(SIDE)
        for k in range(SIDE):
            send_unless_same(source, target, targets[k], itself[k], base + k, base + slot)
        return [
            pltpu.make_async_remote_copy(
                src_ref=source,
                dst_ref=target,
                send_sem=send_sem.at[base + k],
                recv_sem=recv_sem.at[base + k],
                device_id=twin,
                device_id_type=MESH,
            )
            for k in range(SIDE)
        ]

    joined = (joined_first, joined_second, joined_third)
    lanes = lax.broadcasted_iota(jnp.int32, (2 * ROWS, BLOCK), 1)

    def halves(value):
        top = value.astype(jnp.bfloat16)
        return top, (value - top.astype(jnp.float32)).astype(jnp.bfloat16)

    def prepare(level):
        for load in front_loads[level]:
            load.wait()
        for i in range(RED):
            parts = [(front_solve, 0, front_inverse[level, i])]
            parts += [(front_push, k, front_coupling[level, i, k]) for k in range(LINKS)]
            for target, k, value in parts:
                top, rest = halves(value)
                cut = slice(k * BLOCK, (k + 1) * BLOCK)
                target[level, i, 0:BLOCK, cut] = top
                target[level, i, BLOCK : 2 * BLOCK, cut] = top
                target[level, i, 2 * BLOCK : 3 * BLOCK, cut] = rest

    def thrice(value, operator):
        top, rest = halves(value)
        return jnp.dot(
            jnp.concatenate([top, rest, top], 1), operator, preferred_element_type=jnp.float32
        )

    def eliminate(level, block_at):
        _, _, links, _, result = front_data[level]
        live_count = front_rows[level, 0]
        values = []
        for i in range(RED):
            live = (lanes + i * BLOCK < live_count).astype(jnp.float32)
            value = live * thrice(live * block_at(i), front_solve[level, i])
            result[:, i * BLOCK : (i + 1) * BLOCK] = value
            values.append(value)
        pushed = []
        for i in range(RED):
            product = thrice(values[i], front_push[level, i])
            for k in range(LINKS):
                pushed.append((links[i, k], product[:, k * BLOCK : (k + 1) * BLOCK]))
        for j in range(SKELETONS[level]):
            update = jnp.zeros((2 * ROWS, BLOCK), jnp.float32)
            for link, product in pushed:
                update += jnp.where(link == j, 1.0, 0.0) * product
            updated[level, j] = block_at(RED + j) - update

    def join(level, half_at, to):
        half = SKELETONS[level] // 2
        copy = send(
            updated.at[level, pl.ds((1 - half_at) * half, half)],
            joined[level].at[pl.ds(half_at * half, half)],
            to,
        )
        for j in range(half):
            joined[level][half_at * half + j] = updated[level, half_at * half + j]
        return copy

    def ordered(level):
        order = front_data[level][3]
        return lambda k: joined[level][order[0, k]]

    prepare(0)
    first_load.wait()
    eliminate(0, lambda k: first_rows[:, k * BLOCK : (k + 1) * BLOCK])
    prepare(1)
    prepare(2)
    pl.semaphore_wait(
        barrier,
        1
        + (GROUPS - 1)
        + 2 * (SIDE - 1)
        + 4 * SIDE
        - 2 * same_plane.astype(jnp.int32)
        - 2 * same_depth.astype(jnp.int32),
    )
    joining = join(0, core, twin)
    factors = [send(factor_of[k], sibling.at[k], twin) for k in range(3)]
    joining.wait_recv()
    eliminate(1, ordered(0))
    joining = join(1, z_lo % 2, neighbour)
    joining.wait_recv()
    eliminate(2, ordered(1))
    for j in range(SKELETONS[2]):
        joined[2][j] = updated[2, j]
    last_block = ordered(2)
    for k in range(SKELETONS[2]):
        section[k // 2, :, k % 2 * BLOCK : (k % 2 + 1) * BLOCK] = last_block(k)

    mine_at = pl.multiple_of(core * HALF, HALF)
    other_at = pl.multiple_of(other * HALF, HALF)
    kept = pl.ds(pl.multiple_of(core * ROWS, ROWS), ROWS)
    given = pl.ds(pl.multiple_of(other * ROWS, ROWS), ROWS)
    swaps = [
        send(section.at[p, given, :], pieces.at[p, :, pl.ds(mine_at, HALF)], twin)
        for p in range(2)
    ]
    for p in range(2):
        pieces[p, :, pl.ds(mine_at, HALF)] = section[p, kept, :]

    def split(k):
        for source, at in ((own, mine_at), (sibling, other_at)):
            if source is own:
                loads[k].wait()
            else:
                factors[k].wait_recv()
            value = source[k]
            high[k, pl.ds(at, HALF), :], low[k, pl.ds(at, HALF), :] = halves(value)

    def multiply(step, k, transposed):
        top, rest = halves(gathered[step])
        both = jnp.concatenate([top, rest], 0)
        for half in range(2):
            cut = slice(half * HALF, (half + 1) * HALF)
            if transposed:
                right_high, right_low = high[k, cut, :], low[k, cut, :]
            else:
                right_high, right_low = high[k, :, cut], low[k, :, cut]
            dims = (((1,), (1 if transposed else 0,)), ((), ()))
            wide = lax.dot_general(both, right_high, dims, preferred_element_type=jnp.float32)
            thin = lax.dot_general(top, right_low, dims, preferred_element_type=jnp.float32)
            partial[step, :, cut] = wide[:TOTAL] + (wide[TOTAL:] + thin)

    def reduce_leaf(step, meanwhile):
        copies = []
        for n, (a, b) in enumerate(leaf_steps):
            group = lax.rem(x + a, SIDE) * SIDE + lax.rem(z_lo + b, SIDE)
            copies.append(
                send(partial.at[step, rows_of(group)], leaf_in.at[step, n], leaf_targets[n])
            )
        flush(len(pending) - len(copies))
        meanwhile()
        wait_all(copies)
        parts = [partial[step, rows_of(chip_row)]] + [leaf_in[step, n] for n in range(len(copies))]
        while len(parts) > 1:
            parts = [sum(parts[i : i + 2][1:], parts[i]) for i in range(0, len(parts), 2)]
        return parts[0]

    def gather_forward(step, piece):
        copies = turn(piece, moved.at[step - 1, rows_of(z_lo)], depth_forward)
        flush(len(pending) - SIDE)
        wait_all(copies)
        copies = turn(moved.at[step - 1], gathered.at[step, band_of(x)], plane_forward)
        flush(len(pending) - SIDE)
        wait_all(copies)

    def reduce_columns(step, meanwhile):
        at = step - 3
        copies = []
        for d in (2, 1, 3):
            to = lax.rem(y + d, SIDE)
            copies.append(
                send(partial.at[step, band_of(to)], first_in.at[at, d - 1], around("y", d))
            )
        flush(len(pending) - len(copies))
        meanwhile()
        wait_all(copies)
        total = partial[step, band_of(y)]
        first_sum[at] = total + first_in[at, 0] + (first_in[at, 1] + first_in[at, 2])

    def reduce_backward(step):
        at = step - 3
        targets, itself, slot = depth_backward
        base = take(SIDE)
        for k in range(SIDE):
            send_unless_same(
                first_sum.at[at, k * ROWS : (k + 1) * ROWS],
                second_in.at[at, slot],
                targets[k],
                itself[k],
                base + k,
                base + slot,
            )
        flush(len(pending) - SIDE)
        for k in range(SIDE):
            pltpu.make_async_remote_copy(
                src_ref=second_in.at[at, k],
                dst_ref=second_in.at[at, k],
                send_sem=send_sem.at[base + k],
                recv_sem=recv_sem.at[base + k],
                device_id=twin,
                device_id_type=MESH,
            ).wait_recv()
        return (second_in[at, 0] + second_in[at, 1]) + (second_in[at, 2] + second_in[at, 3])

    def gather_backward(step, piece, meanwhile):
        at = step - 4
        copies = [
            send(piece, quarter.at[at, rows_of(z_lo)], around("z_lo", d)) for d in (2, 3, 1)
        ]
        quarter[at, rows_of(z_lo)] = piece[...]
        flush(len(pending) - len(copies))
        wait_all(copies)
        copies = turn(quarter.at[at], gathered.at[step, band_of(y)], plane_backward)
        flush(len(pending) - SIDE)
        meanwhile()
        wait_all(copies)

    def give_result(source, panel):
        copy = send(source.at[:, pl.ds(other_at, HALF)], final_in.at[panel], twin)
        out[kept, panel * HALF : (panel + 1) * HALF] = source[:, pl.ds(mine_at, HALF)]
        return copy

    def take_result(copy, panel):
        copy.wait_recv()
        out[given, panel * HALF : (panel + 1) * HALF] = final_in[panel]

    def nothing():
        pass

    wait_all(swaps)
    copies = [
        send(pieces.at[0], gathered.at[0, rows_of(col)], around("z_hi", d)) for d in (2, 1, 3)
    ]
    n = take(1)
    sinking = send_unless_same(pieces.at[1], turned.at[0], sunk, same_depth, n, n)
    gathered[0, rows_of(col)] = pieces[0]
    split(0)
    wait_all(copies)
    band = gathered.at[0, band_of(y)]
    copies = [send(band, band, around("y", d)) for d in (2, 1, 3)]
    flush(len(pending) - len(copies))
    wait_all(copies)

    multiply(0, 0, False)
    solved[0] = reduce_leaf(0, lambda: split(1))
    n = take(1)
    crossing = send_unless_same(solved.at[0], crossed, flipped, same_plane, n, n)
    gather_forward(1, solved.at[0])

    multiply(1, 1, False)
    turning = []

    def turn_on():
        split(2)
        sinking.wait_recv()
        n = take(1)
        turning.append(
            send_unless_same(turned.at[0], turned.at[1], flipped, same_plane, n, n)
        )

    total = reduce_leaf(1, turn_on)
    turning[0].wait_recv()
    solved[1] = turned[1] - total
    gather_forward(2, solved.at[1])

    multiply(2, 2, False)
    solved[2] = reduce_leaf(2, nothing)
    copies = [send(solved.at[2], gathered.at[3, rows_of(chip_row)], to) for to in leaf_targets]
    gathered[3, rows_of(chip_row)] = solved[2]
    flush(len(pending) - len(copies))
    wait_all(copies)

    multiply(3, 2, True)
    reduce_columns(3, nothing)
    solved[3] = reduce_backward(3)
    n = take(1)
    lifting = send_unless_same(solved.at[3], solved.at[4], sunk, same_depth, n, n)
    gather_backward(4, solved.at[3], nothing)

    multiply(4, 1, True)
    reduce_columns(4, nothing)
    total = reduce_backward(4)
    crossing.wait_recv()
    solved[5] = crossed[...] - total
    handed = []

    def hand_last():
        lifting.wait_recv()
        handed.append(give_result(solved.at[4], 1))

    gather_backward(5, solved.at[5], hand_last)

    multiply(5, 0, True)
    reduce_columns(5, nothing)
    copies = []
    for d in (2, 1, 3):
        to = lax.rem(z_hi + d, SIDE)
        copies.append(
            send(first_sum.at[2, rows_of(to)], second_in.at[2, d - 1], around("z_hi", d))
        )
    flush(len(pending) - len(copies))
    take_result(handed[0], 1)
    wait_all(copies)
    total = first_sum[2, rows_of(z_hi)]
    solved[6] = total + second_in[2, 0] + (second_in[2, 1] + second_in[2, 2])
    first = give_result(solved.at[6], 0)
    take_result(first, 0)
    flush(len(pending))


def local(*operands):
    f32, bf16 = jnp.float32, jnp.bfloat16
    rhs_rows = operands[0].shape[0]
    vmem = pl.BlockSpec(memory_space=pltpu.VMEM)
    smem = pl.BlockSpec(memory_space=pltpu.SMEM)
    whole = pl.BlockSpec(memory_space=pltpu.HBM)
    outputs = pl.pallas_call(
        solve_kernel,
        out_shape=[jax.ShapeDtypeStruct((rhs_rows, SPAN), f32)] * 4,
        in_specs=[whole] + [whole, whole, smem, smem] * 3 + [smem, whole, whole],
        out_specs=[vmem] * 4,
        scratch_shapes=[
            pltpu.VMEM((2 * ROWS, GROUPS * BLOCK), f32),
            pltpu.VMEM((3, RED, BLOCK, BLOCK), f32),
            pltpu.VMEM((3, RED, LINKS, BLOCK, BLOCK), f32),
            pltpu.VMEM((3, RED, 3 * BLOCK, BLOCK), bf16),
            pltpu.VMEM((3, RED, 3 * BLOCK, LINKS * BLOCK), bf16),
            pltpu.VMEM((3, SKELETONS[0], 2 * ROWS, BLOCK), f32),
            pltpu.VMEM((SKELETONS[0], 2 * ROWS, BLOCK), f32),
            pltpu.VMEM((SKELETONS[1], 2 * ROWS, BLOCK), f32),
            pltpu.VMEM((SKELETONS[2], 2 * ROWS, BLOCK), f32),
            pltpu.VMEM((2, 2 * ROWS, HALF), f32),
            pltpu.VMEM((3, HALF, SPAN), f32),
            pltpu.VMEM((3, HALF, SPAN), f32),
            pltpu.VMEM((3, SPAN, SPAN), bf16),
            pltpu.VMEM((3, SPAN, SPAN), bf16),
            pltpu.VMEM((2, ROWS, SPAN), f32),
            pltpu.VMEM((2, ROWS, SPAN), f32),
            pltpu.VMEM((ROWS, SPAN), f32),
            pltpu.VMEM((2, SIDE * ROWS, SPAN), f32),
            pltpu.VMEM((STEPS, TOTAL, SPAN), f32),
            pltpu.VMEM((STEPS, TOTAL, SPAN), f32),
            pltpu.VMEM((3, GROUPS - 1, ROWS, SPAN), f32),
            pltpu.VMEM((3, SIDE - 1, SIDE * ROWS, SPAN), f32),
            pltpu.VMEM((3, SIDE * ROWS, SPAN), f32),
            pltpu.VMEM((3, SIDE, ROWS, SPAN), f32),
            pltpu.VMEM((2, SIDE * ROWS, SPAN), f32),
            pltpu.VMEM((7, ROWS, SPAN), f32),
            pltpu.VMEM((2, ROWS, HALF), f32),
            pltpu.SemaphoreType.DMA((MESSAGES,)),
            pltpu.SemaphoreType.DMA((MESSAGES,)),
            pltpu.SemaphoreType.DMA((10,)),
        ],
        compiler_params=pltpu.CompilerParams(
            collective_id=0, has_side_effects=True, vmem_limit_bytes=63 << 20
        ),
        name="solve",
    )(*operands)
    return (*outputs[:3], outputs[3].reshape(rhs_rows, 2, HALF))


def solution(mesh):
    in_specs = (
        P("col", "leaf"),
        P("leaf", None, None),
        P("leaf", None, None, None),
        P("leaf", None),
        P("leaf", None),
        P("leaf", None, None),
        P("leaf", None, None, None),
        P("leaf", None),
        P("leaf", None),
        P("leaf", None, None),
        P("leaf", None, None, None),
        P("leaf", None),
        P("leaf", None),
        P(None, "leaf"),
        P(None, "leaf", "col"),
        P("leaf", "col"),
    )
    out_specs = (P("col", "leaf"), P("col", "leaf"), P("col", "leaf"), P("col", None, "leaf"))
    return jax.shard_map(local, mesh=mesh, in_specs=in_specs, out_specs=out_specs, check_vma=False)
```

time: 190 us -> 171 us (0.900)
  starting transfers between devices: 10.8 us -> 0 us
  Pallas kernels: 158 us -> 166 us
  local copies, waits for them, and re-layouts: 9.98 us -> 4.87 us
  matrix products: 4.6 us -> 0 us
  waiting for transfers between devices: 2.61 us -> 0 us
  other arithmetic: 2.17 us -> 0 us
    ppermute x2 -> x0, starting transfers between devices: 10.8 us -> none  [partner(): return lax.ppermute(block, axis, route)]
    pallas_call x1, Pallas kernels: 158 us -> 166 us  [local(): pl.pallas_call(solve_kernel, out_shape=[jax.ShapeDtypeStruct((rhs_rows, S...]
    dot_general x9 -> x0, matrix products: 4.6 us -> none  [the longest x3 1.92 us: eliminate(): jnp.einsum('rib,iba->ria', redundant * live_rows, inverse, precision=lax....]
    ppermute x2 -> x0, waiting for transfers between devices: 2.61 us -> none  [partner(): return lax.ppermute(block, axis, route)]
    convert_element_type x1 -> x0, other arithmetic: 2.01 us -> none  [eliminate(): live_rows = (positions < live_count).astype(jnp.float32)]
    unnamed x37 -> x10, local copies, waits for them, and re-layouts: 4.54 us -> 3.47 us
  transfers between devices with their start and end apart: 2 -> 0, of which waited for: 1 -> 0; matrix products, arithmetic and copies ran while one was open for 1% -> 0% of each run, Pallas kernels for 0% -> 0%
where the time goes in v2:
time: 171 us
  Pallas kernels  166 us (97%)
  local copies, waits for them, and re-layouts  4.87 us (3%)
    pallas_call x1, Pallas kernels, local(): pl.pallas_call(solve_kernel, out_shape=[jax.ShapeDtypeStruct((rhs_rows, S...  166 us
    unnamed x10, local copies, waits for them, and re-layouts  3.47 us

profile of v2, /device:TPU:1, one launch (start us, length us, event | category | flops | bytes accessed | tf_op | source)
XLA Modules:
  0.0 171.1 jit_solution(7311720558910623563)
XLA Ops:
  0.6 1.3 copy.20.front_rows
  1.9 165.6 %solve.1 = (f32[16,512]{1,0:T(8,128)}, f32[16,512]{1,0:T(8,128)}, f32[16,512]{1,0:T(8,128)}, f32[16,512]{1,0:T(8,128)}) custom-call(f32[16,2048]{1,0:T(8,128)} %right_sides.1, f32[4,128,128]{2,1,0:T(8,128)} %inverse_first.1, f32[4,3,128,128]{3,2,1,0:T(8,128)} %coupling_first.1, s32[4,3]{1,0:T(4,128)} %links_first.1, s32[1,12]{1,0:T(1,128)} %order_first.1, ...), custom_call_target="tpu_custom_call" | custom-call | tf_op jit(solution)/shard_map/solve/pallas_call | solution.py:542
  167.5 0.0 copy-start.2
  167.5 1.4 reshape.11
  168.9 0.0 copy-done.2
  168.9 0.0 copy-start.1
  168.9 0.6 copy.24
  169.6 0.2 copy-done.1
  169.7 0.0 copy-start
  169.7 0.6 copy.25
  170.3 0.2 copy-done
  170.5 0.6 copy.26
Async XLA Ops:
  167.5 1.4 copy-start.2
  168.9 0.8 copy-start.1
  169.7 0.8 copy-start

commit v3 on v2

--- a/solution.py
+++ b/solution.py
@@ -77,7 +77,6 @@
     first_in,
     first_sum,
     second_in,
-    quarter,
     solved,
     final_in,
     send_sem,
@@ -157,18 +156,30 @@
     def greet(to):
         pl.semaphore_signal(barrier, inc=1, device_id=to, device_id_type=MESH)
 
-    greet(twin)
-    for to in leaf_targets:
-        greet(to)
-    for axis in ("y", "z_hi"):
-        for step in range(1, SIDE):
-            greet(around(axis, step))
     for targets, itself, _ in (depth_forward, depth_backward, plane_forward, plane_backward):
         for k in range(SIDE):
 
             @pl.when(jnp.logical_not(itself[k]))
             def _():
                 greet(targets[k])
+
+    for axis in ("z_hi", "y"):
+        for step in (2, 1, 3):
+            greet(around(axis, step))
+    for to in leaf_targets:
+        greet(to)
+    greet(twin)
+
+    def meet():
+        pl.semaphore_wait(
+            barrier,
+            1
+            + (GROUPS - 1)
+            + 2 * (SIDE - 1)
+            + 4 * SIDE
+            - 2 * same_plane.astype(jnp.int32)
+            - 2 * same_depth.astype(jnp.int32),
+        )
 
     used = [0]
     pending = []
@@ -271,7 +282,7 @@
 
     def eliminate(level, block_at):
         _, _, links, _, result = front_data[level]
-        live_count = front_rows[level, 0]
+        live_count = front_rows[0, level]
         values = []
         for i in range(RED):
             live = (lanes + i * BLOCK < live_count).astype(jnp.float32)
@@ -309,15 +320,7 @@
     eliminate(0, lambda k: first_rows[:, k * BLOCK : (k + 1) * BLOCK])
     prepare(1)
     prepare(2)
-    pl.semaphore_wait(
-        barrier,
-        1
-        + (GROUPS - 1)
-        + 2 * (SIDE - 1)
-        + 4 * SIDE
-        - 2 * same_plane.astype(jnp.int32)
-        - 2 * same_depth.astype(jnp.int32),
-    )
+    meet()
     joining = join(0, core, twin)
     factors = [send(factor_of[k], sibling.at[k], twin) for k in range(3)]
     joining.wait_recv()
@@ -388,55 +391,47 @@
         flush(len(pending) - SIDE)
         wait_all(copies)
 
-    def reduce_columns(step, meanwhile):
-        at = step - 3
-        copies = []
-        for d in (2, 1, 3):
-            to = lax.rem(y + d, SIDE)
-            copies.append(
-                send(partial.at[step, band_of(to)], first_in.at[at, d - 1], around("y", d))
-            )
-        flush(len(pending) - len(copies))
-        meanwhile()
-        wait_all(copies)
-        total = partial[step, band_of(y)]
-        first_sum[at] = total + first_in[at, 0] + (first_in[at, 1] + first_in[at, 2])
-
-    def reduce_backward(step):
-        at = step - 3
-        targets, itself, slot = depth_backward
+    def reduce_turned(at, pieces_at, slots, route, meanwhile):
+        targets, itself, slot = route
         base = take(SIDE)
         for k in range(SIDE):
             send_unless_same(
-                first_sum.at[at, k * ROWS : (k + 1) * ROWS],
-                second_in.at[at, slot],
-                targets[k],
-                itself[k],
-                base + k,
-                base + slot,
+                pieces_at(k), slots.at[at, slot], targets[k], itself[k], base + k, base + slot
             )
         flush(len(pending) - SIDE)
+        meanwhile()
         for k in range(SIDE):
             pltpu.make_async_remote_copy(
-                src_ref=second_in.at[at, k],
-                dst_ref=second_in.at[at, k],
+                src_ref=slots.at[at, k],
+                dst_ref=slots.at[at, k],
                 send_sem=send_sem.at[base + k],
                 recv_sem=recv_sem.at[base + k],
                 device_id=twin,
                 device_id_type=MESH,
             ).wait_recv()
-        return (second_in[at, 0] + second_in[at, 1]) + (second_in[at, 2] + second_in[at, 3])
-
-    def gather_backward(step, piece, meanwhile):
-        at = step - 4
-        copies = [
-            send(piece, quarter.at[at, rows_of(z_lo)], around("z_lo", d)) for d in (2, 3, 1)
-        ]
-        quarter[at, rows_of(z_lo)] = piece[...]
+        return (slots[at, 0] + slots[at, 1]) + (slots[at, 2] + slots[at, 3])
+
+    def reduce_backward(step, meanwhile):
+        at = step - 3
+        first_sum[at] = reduce_turned(
+            at,
+            lambda k: partial.at[step, k * SIDE * ROWS : (k + 1) * SIDE * ROWS],
+            first_in,
+            plane_backward,
+            meanwhile,
+        )
+        return reduce_turned(
+            at,
+            lambda k: first_sum.at[at, k * ROWS : (k + 1) * ROWS],
+            second_in,
+            depth_backward,
+            nothing,
+        )
+
+    def gather_leaf(step, piece, meanwhile):
+        copies = [send(piece, gathered.at[step, rows_of(chip_row)], to) for to in leaf_targets]
+        gathered[step, rows_of(chip_row)] = piece[...]
         flush(len(pending) - len(copies))
-        wait_all(copies)
-        copies = turn(quarter.at[at], gathered.at[step, band_of(y)], plane_backward)
-        flush(len(pending) - SIDE)
         meanwhile()
         wait_all(copies)
 
@@ -468,8 +463,6 @@
 
     multiply(0, 0, False)
     solved[0] = reduce_leaf(0, lambda: split(1))
-    n = take(1)
-    crossing = send_unless_same(solved.at[0], crossed, flipped, same_plane, n, n)
     gather_forward(1, solved.at[0])
 
     multiply(1, 1, False)
@@ -490,33 +483,41 @@
 
     multiply(2, 2, False)
     solved[2] = reduce_leaf(2, nothing)
-    copies = [send(solved.at[2], gathered.at[3, rows_of(chip_row)], to) for to in leaf_targets]
-    gathered[3, rows_of(chip_row)] = solved[2]
+    gather_leaf(3, solved.at[2], nothing)
+
+    multiply(3, 2, True)
+    solved[3] = reduce_backward(3, nothing)
+    n = take(1)
+    sinking_last = send_unless_same(solved.at[3], solved.at[4], sunk, same_depth, n, n)
+    gather_leaf(4, solved.at[3], nothing)
+
+    multiply(4, 1, True)
+    handed = []
+
+    def turn_last():
+        sinking_last.wait_recv()
+        n = take(1)
+        handed.append(send_unless_same(solved.at[4], crossed, flipped, same_plane, n, n))
+
+    def hand_last():
+        handed[0].wait_recv()
+        handed.append(give_result(crossed, 1))
+
+    total = reduce_backward(4, turn_last)
+    solved[5] = solved[0] - total
+    gather_leaf(5, solved.at[5], hand_last)
+
+    multiply(5, 0, True)
+    copies = []
+    for d in (2, 1, 3):
+        to = lax.rem(y + d, SIDE)
+        copies.append(
+            send(partial.at[5, band_of(to)], first_in.at[2, d - 1], around("y", d))
+        )
     flush(len(pending) - len(copies))
     wait_all(copies)
-
-    multiply(3, 2, True)
-    reduce_columns(3, nothing)
-    solved[3] = reduce_backward(3)
-    n = take(1)
-    lifting = send_unless_same(solved.at[3], solved.at[4], sunk, same_depth, n, n)
-    gather_backward(4, solved.at[3], nothing)
-
-    multiply(4, 1, True)
-    reduce_columns(4, nothing)
-    total = reduce_backward(4)
-    crossing.wait_recv()
-    solved[5] = crossed[...] - total
-    handed = []
-
-    def hand_last():
-        lifting.wait_recv()
-        handed.append(give_result(solved.at[4], 1))
-
-    gather_backward(5, solved.at[5], hand_last)
-
-    multiply(5, 0, True)
-    reduce_columns(5, nothing)
+    total = partial[5, band_of(y)]
+    first_sum[2] = total + first_in[2, 0] + (first_in[2, 1] + first_in[2, 2])
     copies = []
     for d in (2, 1, 3):
         to = lax.rem(z_hi + d, SIDE)
@@ -524,13 +525,21 @@
             send(first_sum.at[2, rows_of(to)], second_in.at[2, d - 1], around("z_hi", d))
         )
     flush(len(pending) - len(copies))
-    take_result(handed[0], 1)
+    take_result(handed[1], 1)
     wait_all(copies)
     total = first_sum[2, rows_of(z_hi)]
     solved[6] = total + second_in[2, 0] + (second_in[2, 1] + second_in[2, 2])
     first = give_result(solved.at[6], 0)
     take_result(first, 0)
     flush(len(pending))
+
+
+def hand_over(first, second, third, root, out_first, out_second, out_third, out_root):
+    out_first[...] = first[...]
+    out_second[...] = second[...]
+    out_third[...] = third[...]
+    for p in range(2):
+        out_root[:, p, :] = root[:, p * HALF : (p + 1) * HALF]
 
 
 def local(*operands):
@@ -566,10 +575,9 @@
             pltpu.VMEM((STEPS, TOTAL, SPAN), f32),
             pltpu.VMEM((STEPS, TOTAL, SPAN), f32),
             pltpu.VMEM((3, GROUPS - 1, ROWS, SPAN), f32),
-            pltpu.VMEM((3, SIDE - 1, SIDE * ROWS, SPAN), f32),
+            pltpu.VMEM((3, SIDE, SIDE * ROWS, SPAN), f32),
             pltpu.VMEM((3, SIDE * ROWS, SPAN), f32),
             pltpu.VMEM((3, SIDE, ROWS, SPAN), f32),
-            pltpu.VMEM((2, SIDE * ROWS, SPAN), f32),
             pltpu.VMEM((7, ROWS, SPAN), f32),
             pltpu.VMEM((2, ROWS, HALF), f32),
             pltpu.SemaphoreType.DMA((MESSAGES,)),
@@ -580,8 +588,15 @@
             collective_id=0, has_side_effects=True, vmem_limit_bytes=63 << 20
         ),
         name="solve",
-    )(*operands)
-    return (*outputs[:3], outputs[3].reshape(rhs_rows, 2, HALF))
+    )(*operands[:13], operands[13].T, *operands[14:])
+    shapes = [jax.ShapeDtypeStruct((rhs_rows, SPAN), f32)] * 3
+    return pl.pallas_call(
+        hand_over,
+        out_shape=[*shapes, jax.ShapeDtypeStruct((rhs_rows, 2, HALF), f32)],
+        in_specs=[vmem] * 4,
+        out_specs=[vmem] * 4,
+        name="hand_over",
+    )(*outputs)
 
 
 def solution(mesh):

time: 171 us -> 169 us (0.988)
  local copies, waits for them, and re-layouts: 4.87 us -> 0 us
  Pallas kernels: 166 us -> 168 us
    unnamed x10 -> x0, local copies, waits for them, and re-layouts: 3.47 us -> none
where the time goes in v3:
time: 169 us
  Pallas kernels  168 us (99%)
    pallas_call x1, Pallas kernels, local(): pl.pallas_call(solve_kernel, out_shape=[jax.ShapeDtypeStruct((rhs_rows, S...  167 us

profile of v3, /device:TPU:1, one launch (start us, length us, event | category | flops | bytes accessed | tf_op | source)
XLA Modules:
  0.0 169.0 jit_solution(4400824589386155826)
XLA Ops:
  0.6 166.9 %solve.1 = (f32[16,512]{1,0:T(8,128)}, f32[16,512]{1,0:T(8,128)}, f32[16,512]{1,0:T(8,128)}, f32[16,512]{1,0:T(8,128)}) custom-call(f32[16,2048]{1,0:T(8,128)} %right_sides.1, f32[4,128,128]{2,1,0:T(8,128)} %inverse_first.1, f32[4,3,128,128]{3,2,1,0:T(8,128)} %coupling_first.1, s32[4,3]{1,0:T(4,128)} %links_first.1, s32[1,12]{1,0:T(1,128)} %order_first.1, ...), custom_call_target="tpu_custom_call" | custom-call | tf_op jit(solution)/shard_map/solve/pallas_call | solution.py:551
  167.6 1.5 hand_over.1

commit v4 on v3

--- a/solution.py
+++ b/solution.py
@@ -17,7 +17,7 @@
 LINKS = 3
 SKELETONS = (12, 8, 4)
 STEPS = 6
-MESSAGES = 160
+MESSAGES = 240
 
 
 def device(x, z_lo, core, y, z_hi):
@@ -254,6 +254,20 @@
             for k in range(SIDE)
         ]
 
+    def wait_slots(base, slots):
+        for k in range(SIDE):
+            pltpu.make_async_remote_copy(
+                src_ref=slots.at[k],
+                dst_ref=slots.at[k],
+                send_sem=send_sem.at[base + k],
+                recv_sem=recv_sem.at[base + k],
+                device_id=twin,
+                device_id_type=MESH,
+            ).wait_recv()
+
+    def sum_slots(slots, *at):
+        return (slots[*at, 0] + slots[*at, 1]) + (slots[*at, 2] + slots[*at, 3])
+
     joined = (joined_first, joined_second, joined_third)
     lanes = lax.broadcasted_iota(jnp.int32, (2 * ROWS, BLOCK), 1)
 
@@ -386,47 +400,52 @@
     def gather_forward(step, piece):
         copies = turn(piece, moved.at[step - 1, rows_of(z_lo)], depth_forward)
         flush(len(pending) - SIDE)
-        wait_all(copies)
-        copies = turn(moved.at[step - 1], gathered.at[step, band_of(x)], plane_forward)
-        flush(len(pending) - SIDE)
-        wait_all(copies)
-
-    def reduce_turned(at, pieces_at, slots, route, meanwhile):
-        targets, itself, slot = route
-        base = take(SIDE)
+        onward = []
         for k in range(SIDE):
+            copies[k].wait_recv()
+            onward += turn(
+                moved.at[step - 1, k * ROWS : (k + 1) * ROWS],
+                gathered.at[step, rows_of(x * SIDE + k)],
+                plane_forward,
+            )
+        flush(len(pending) - len(onward))
+        wait_all(onward)
+
+    def reduce_backward(step, meanwhile):
+        at = step - 3
+        arriving = []
+        for k in range(SIDE):
+            targets, itself, slot = plane_backward
+            base = take(SIDE)
+            for band in range(SIDE):
+                row = (band * SIDE + k) * ROWS
+                send_unless_same(
+                    partial.at[step, row : row + ROWS],
+                    first_in.at[at, k, slot],
+                    targets[band],
+                    itself[band],
+                    base + band,
+                    base + slot,
+                )
+            arriving.append(base)
+        flush(len(pending) - GROUPS)
+        meanwhile()
+        targets, itself, slot = depth_backward
+        last = take(SIDE)
+        for k in range(SIDE):
+            wait_slots(arriving[k], first_in.at[at, k])
+            first_sum[at, k * ROWS : (k + 1) * ROWS] = sum_slots(first_in, at, k)
             send_unless_same(
-                pieces_at(k), slots.at[at, slot], targets[k], itself[k], base + k, base + slot
+                first_sum.at[at, k * ROWS : (k + 1) * ROWS],
+                second_in.at[at, slot],
+                targets[k],
+                itself[k],
+                last + k,
+                last + slot,
             )
         flush(len(pending) - SIDE)
-        meanwhile()
-        for k in range(SIDE):
-            pltpu.make_async_remote_copy(
-                src_ref=slots.at[at, k],
-                dst_ref=slots.at[at, k],
-                send_sem=send_sem.at[base + k],
-                recv_sem=recv_sem.at[base + k],
-                device_id=twin,
-                device_id_type=MESH,
-            ).wait_recv()
-        return (slots[at, 0] + slots[at, 1]) + (slots[at, 2] + slots[at, 3])
-
-    def reduce_backward(step, meanwhile):
-        at = step - 3
-        first_sum[at] = reduce_turned(
-            at,
-            lambda k: partial.at[step, k * SIDE * ROWS : (k + 1) * SIDE * ROWS],
-            first_in,
-            plane_backward,
-            meanwhile,
-        )
-        return reduce_turned(
-            at,
-            lambda k: first_sum.at[at, k * ROWS : (k + 1) * ROWS],
-            second_in,
-            depth_backward,
-            nothing,
-        )
+        wait_slots(last, second_in.at[at])
+        return sum_slots(second_in, at)
 
     def gather_leaf(step, piece, meanwhile):
         copies = [send(piece, gathered.at[step, rows_of(chip_row)], to) for to in leaf_targets]
@@ -454,12 +473,16 @@
     n = take(1)
     sinking = send_unless_same(pieces.at[1], turned.at[0], sunk, same_depth, n, n)
     gathered[0, rows_of(col)] = pieces[0]
+    onward = [
+        send(pieces.at[0], gathered.at[0, rows_of(col)], around("y", d)) for d in (2, 1, 3)
+    ]
     split(0)
-    wait_all(copies)
-    band = gathered.at[0, band_of(y)]
-    copies = [send(band, band, around("y", d)) for d in (2, 1, 3)]
-    flush(len(pending) - len(copies))
-    wait_all(copies)
+    for n, step in ((1, 1), (2, 3), (0, 2)):
+        copies[n].wait_recv()
+        band = gathered.at[0, rows_of(y * SIDE + lax.rem(z_hi + SIDE - step, SIDE))]
+        onward += [send(band, band, around("y", d)) for d in (2, 1, 3)]
+    flush(len(pending) - len(onward))
+    wait_all(onward)
 
     multiply(0, 0, False)
     solved[0] = reduce_leaf(0, lambda: split(1))
@@ -508,26 +531,41 @@
     gather_leaf(5, solved.at[5], hand_last)
 
     multiply(5, 0, True)
+    order = (2, 1, 3, 0)
+    arriving = []
+    for n, d in enumerate(order):
+        group = lax.rem(z_hi + d, SIDE)
+        arriving.append(
+            [
+                send(
+                    partial.at[5, rows_of(lax.rem(y + e, SIDE) * SIDE + group)],
+                    first_in.at[2, n, e - 1],
+                    around("y", e),
+                )
+                for e in (2, 1, 3)
+            ]
+        )
+    flush(len(pending) - 4 * (SIDE - 1))
     copies = []
-    for d in (2, 1, 3):
-        to = lax.rem(y + d, SIDE)
-        copies.append(
-            send(partial.at[5, band_of(to)], first_in.at[2, d - 1], around("y", d))
-        )
-    flush(len(pending) - len(copies))
-    wait_all(copies)
-    total = partial[5, band_of(y)]
-    first_sum[2] = total + first_in[2, 0] + (first_in[2, 1] + first_in[2, 2])
-    copies = []
-    for d in (2, 1, 3):
-        to = lax.rem(z_hi + d, SIDE)
-        copies.append(
-            send(first_sum.at[2, rows_of(to)], second_in.at[2, d - 1], around("z_hi", d))
-        )
+    for n, d in enumerate(order):
+        group = lax.rem(z_hi + d, SIDE)
+        wait_all(arriving[n])
+        total = partial[5, rows_of(y * SIDE + group)]
+        first_sum[2, n * ROWS : (n + 1) * ROWS] = (
+            total + first_in[2, n, 0] + (first_in[2, n, 1] + first_in[2, n, 2])
+        )
+        if d:
+            copies.append(
+                send(
+                    first_sum.at[2, n * ROWS : (n + 1) * ROWS],
+                    second_in.at[2, d - 1],
+                    around("z_hi", d),
+                )
+            )
     flush(len(pending) - len(copies))
     take_result(handed[1], 1)
     wait_all(copies)
-    total = first_sum[2, rows_of(z_hi)]
+    total = first_sum[2, 3 * ROWS : 4 * ROWS]
     solved[6] = total + second_in[2, 0] + (second_in[2, 1] + second_in[2, 2])
     first = give_result(solved.at[6], 0)
     take_result(first, 0)
@@ -575,7 +613,7 @@
             pltpu.VMEM((STEPS, TOTAL, SPAN), f32),
             pltpu.VMEM((STEPS, TOTAL, SPAN), f32),
             pltpu.VMEM((3, GROUPS - 1, ROWS, SPAN), f32),
-            pltpu.VMEM((3, SIDE, SIDE * ROWS, SPAN), f32),
+            pltpu.VMEM((3, SIDE, SIDE, ROWS, SPAN), f32),
             pltpu.VMEM((3, SIDE * ROWS, SPAN), f32),
             pltpu.VMEM((3, SIDE, ROWS, SPAN), f32),
             pltpu.VMEM((7, ROWS, SPAN), f32),

time: 169 us -> 160 us (0.947)
  Pallas kernels: 168 us -> 159 us
    pallas_call x1, Pallas kernels: 167 us -> 158 us  [local(): pl.pallas_call(solve_kernel, out_shape=[jax.ShapeDtypeStruct((rhs_rows, S...]
where the time goes in v4:
time: 160 us
  Pallas kernels  159 us (99%)
    pallas_call x1, Pallas kernels, local(): pl.pallas_call(solve_kernel, out_shape=[jax.ShapeDtypeStruct((rhs_rows, S...  158 us

profile of v4, /device:TPU:1, one launch (start us, length us, event | category | flops | bytes accessed | tf_op | source)
XLA Modules:
  0.0 159.9 jit_solution(8196252797433523227)
XLA Ops:
  0.6 157.8 %solve.1 = (f32[16,512]{1,0:T(8,128)}, f32[16,512]{1,0:T(8,128)}, f32[16,512]{1,0:T(8,128)}, f32[16,512]{1,0:T(8,128)}) custom-call(f32[16,2048]{1,0:T(8,128)} %right_sides.1, f32[4,128,128]{2,1,0:T(8,128)} %inverse_first.1, f32[4,3,128,128]{3,2,1,0:T(8,128)} %coupling_first.1, s32[4,3]{1,0:T(4,128)} %links_first.1, s32[1,12]{1,0:T(1,128)} %order_first.1, ...), custom_call_target="tpu_custom_call" | custom-call | tf_op jit(solution)/shard_map/solve/pallas_call | solution.py:589
  158.5 1.5 hand_over.1

commit v5 on v4

--- a/solution.py
+++ b/solution.py
@@ -17,6 +17,7 @@
 LINKS = 3
 SKELETONS = (12, 8, 4)
 STEPS = 6
+ORDER = (2, 1, 3, 0)
 MESSAGES = 240
 
 
@@ -105,23 +106,23 @@
         device(lax.rem(x + a, SIDE), lax.rem(z_lo + b, SIDE), core, y, z_hi) for a, b in leaf_steps
     ]
     depth_forward = (
-        [device(x, z_hi, core, y, k) for k in range(SIDE)],
-        [jnp.logical_and(same_depth, z_hi == k) for k in range(SIDE)],
+        [device(x, z_hi, core, y, lax.rem(z_hi + d, SIDE)) for d in ORDER],
+        same_depth,
         z_lo,
     )
     depth_backward = (
-        [device(x, k, core, y, z_lo) for k in range(SIDE)],
-        [jnp.logical_and(same_depth, z_lo == k) for k in range(SIDE)],
+        [device(x, lax.rem(z_lo + d, SIDE), core, y, z_lo) for d in ORDER],
+        same_depth,
         z_hi,
     )
     plane_forward = (
-        [device(y, z_lo, core, k, z_hi) for k in range(SIDE)],
-        [jnp.logical_and(same_plane, y == k) for k in range(SIDE)],
+        [device(y, z_lo, core, lax.rem(y + d, SIDE), z_hi) for d in ORDER],
+        same_plane,
         x,
     )
     plane_backward = (
-        [device(k, z_lo, core, x, z_hi) for k in range(SIDE)],
-        [jnp.logical_and(same_plane, x == k) for k in range(SIDE)],
+        [device(lax.rem(x + d, SIDE), z_lo, core, x, z_hi) for d in ORDER],
+        same_plane,
         y,
     )
 
@@ -157,11 +158,12 @@
         pl.semaphore_signal(barrier, inc=1, device_id=to, device_id_type=MESH)
 
     for targets, itself, _ in (depth_forward, depth_backward, plane_forward, plane_backward):
-        for k in range(SIDE):
-
-            @pl.when(jnp.logical_not(itself[k]))
-            def _():
-                greet(targets[k])
+        for to in targets[:-1]:
+            greet(to)
+
+        @pl.when(jnp.logical_not(itself))
+        def _():
+            greet(targets[-1])
 
     for axis in ("z_hi", "y"):
         for step in (2, 1, 3):
@@ -212,6 +214,11 @@
             device_id_type=MESH,
         )
 
+        if itself is None:
+            remote.start()
+            pending.append(remote.wait_send)
+            return remote
+
         @pl.when(jnp.logical_not(itself))
         def _():
             remote.start()
@@ -240,8 +247,10 @@
     def turn(source, target, route):
         targets, itself, slot = route
         base = take(SIDE)
-        for k in range(SIDE):
-            send_unless_same(source, target, targets[k], itself[k], base + k, base + slot)
+        for n, d in enumerate(ORDER):
+            send_unless_same(
+                source, target, targets[n], None if d else itself, base + n, base + slot
+            )
         return [
             pltpu.make_async_remote_copy(
                 src_ref=source,
@@ -414,17 +423,17 @@
     def reduce_backward(step, meanwhile):
         at = step - 3
         arriving = []
-        for k in range(SIDE):
+        for i, shift in enumerate(ORDER):
             targets, itself, slot = plane_backward
             base = take(SIDE)
-            for band in range(SIDE):
-                row = (band * SIDE + k) * ROWS
+            for n, d in enumerate(ORDER):
+                group = lax.rem(x + d, SIDE) * SIDE + lax.rem(z_lo + shift, SIDE)
                 send_unless_same(
-                    partial.at[step, row : row + ROWS],
-                    first_in.at[at, k, slot],
-                    targets[band],
-                    itself[band],
-                    base + band,
+                    partial.at[step, rows_of(group)],
+                    first_in.at[at, i, slot],
+                    targets[n],
+                    None if d else itself,
+                    base + n,
                     base + slot,
                 )
             arriving.append(base)
@@ -439,7 +448,7 @@
                 first_sum.at[at, k * ROWS : (k + 1) * ROWS],
                 second_in.at[at, slot],
                 targets[k],
-                itself[k],
+                None if ORDER[k] else itself,
                 last + k,
                 last + slot,
             )

time: 160 us -> 158 us (0.988)
  Pallas kernels: 159 us -> 156 us
    pallas_call x1, Pallas kernels: 158 us -> 155 us  [local(): pl.pallas_call(solve_kernel, out_shape=[jax.ShapeDtypeStruct((rhs_rows, S...]
where the time goes in v5:
time: 158 us; the launch traced here: 157 us
  Pallas kernels  156 us (99%)
    pallas_call x1, Pallas kernels, local(): pl.pallas_call(solve_kernel, out_shape=[jax.ShapeDtypeStruct((rhs_rows, S...  155 us

profile of v5, /device:TPU:1, one launch (start us, length us, event | category | flops | bytes accessed | tf_op | source)
XLA Modules:
  0.0 156.9 jit_solution(8266296685024015024)
XLA Ops:
  0.6 154.8 %solve.1 = (f32[16,512]{1,0:T(8,128)}, f32[16,512]{1,0:T(8,128)}, f32[16,512]{1,0:T(8,128)}, f32[16,512]{1,0:T(8,128)}) custom-call(f32[16,2048]{1,0:T(8,128)} %right_sides.1, f32[4,128,128]{2,1,0:T(8,128)} %inverse_first.1, f32[4,3,128,128]{3,2,1,0:T(8,128)} %coupling_first.1, s32[4,3]{1,0:T(4,128)} %links_first.1, s32[1,12]{1,0:T(1,128)} %order_first.1, ...), custom_call_target="tpu_custom_call" | custom-call | tf_op jit(solution)/shard_map/solve/pallas_call | solution.py:598
  155.5 1.5 hand_over.1
